TPU v7x, 32 devices: a whole 2x2x4 slice. The times are simulated.
32 devices in a mesh: fsdp: 4 (over z), sp: 8 (over y, x, core).
Axes of the slice: x: 2, y: 2, z: 4, core: 2. Of those that a mesh axis runs over, the one named last changes fastest.
Arguments:
- tokens: bfloat16 [4096, 2048], P(('fsdp', 'sp')), may hold values from -6 to 6
- segments: int32 [4, 1024], P('fsdp'), may hold values from 0 to 7, never falling along the last dimension, each value on 1 to 512 neighbouring positions
- prenorm: bfloat16 [2048], P('fsdp'), may hold values from 0.099609375 to 1.8984375
- query_proj: bfloat16 [2048, 2048], P('fsdp'), may hold values from -0.125 to 0.125
- key_projection: bfloat16 [2048, 1024], P('fsdp'), may hold values from -0.125 to 0.125
- value_projection: bfloat16 [2048, 1024], P('fsdp'), may hold values from -0.125 to 0.125
- query_norm: bfloat16 [128], replicated, may hold values from 0.099609375 to 1.8984375
- key_norm_gain: bfloat16 [128], replicated, may hold values from 0.099609375 to 1.8984375
- output_proj: bfloat16 [2048, 2048], P('fsdp'), may hold values from -1 to 1
- postnorm: bfloat16 [2048], P('fsdp'), may hold values from 0.099609375 to 1.8984375
- gate_proj: bfloat16 [2048, 6144], P('fsdp'), may hold values from -0.125 to 0.125
- up_proj: bfloat16 [2048, 6144], P('fsdp'), may hold values from -0.125 to 0.125
- down_proj: bfloat16 [2048, 6144], P('fsdp'), may hold values from -0.078125 to 0.078125
- out_grad: bfloat16 [4096, 2048], P(('fsdp', 'sp')), may hold values from -6 to 6
Outputs:
- block_out: bfloat16 [4096, 2048], P(('fsdp', 'sp'))
- input_grad: bfloat16 [4096, 2048], P(('fsdp', 'sp'))
- grad_prenorm: float32 [2048], P('fsdp')
- grad_query: float32 [2048, 2048], P('fsdp')
- grad_key: float32 [2048, 1024], P('fsdp')
- grad_value: float32 [2048, 1024], P('fsdp')
- grad_querynorm: float32 [128], replicated
- grad_keynorm: float32 [128], replicated
- grad_output: float32 [2048, 2048], P('fsdp')
- grad_postnorm: float32 [2048], P('fsdp')
- grad_gate: float32 [2048, 6144], P('fsdp')
- grad_up: float32 [2048, 6144], P('fsdp')
- grad_down: float32 [2048, 6144], P('fsdp')
Inputs may be any that keep to these rules, and one draw needn't show every extreme that they name: `segments`: document numbers of a sequence's tokens never fall; each of the 8 documents holds 1 to 512 tokens.
All inputs are finite; a program needn't handle non-finite values.
Results may differ from a plain program's by a relative error of at most 0.018.
Values may be sent and summed in bfloat16 or wider, within the bound.
No kernel may reach another device: no remote copies, remote signals or barrier semaphores. Data moves between devices by JAX's collectives and lax.ppermute only.
A program may use at most 384 MiB of HBM per device.

v0:
```python
import jax
import jax.numpy as jnp
from jax import lax
from jax.sharding import PartitionSpec as P

QUERY_HEADS = 16
KEY_VALUE_HEADS = 8
HEAD_DIMENSION = 128


epsilon = 1e-06
rope_base = 1000000.0
single_precision = jnp.float32
reduced_precision = jnp.bfloat16


def contract_last(left_side, right_side):
    return lax.dot_general(
        left_side, right_side, (((1,), (1,)), ((), ())), preferred_element_type=single_precision
    )


def contract_first(left_side, right_side):
    return lax.dot_general(
        left_side, right_side, (((0,), (0,)), ((), ())), preferred_element_type=single_precision
    )


def rope_tables(places):
    half_dim = HEAD_DIMENSION // 2
    frequency = jnp.power(
        rope_base, -(jnp.arange(half_dim, dtype=single_precision) * (2.0 / HEAD_DIMENSION))
    )
    angles = places[:, None] * frequency[None, :]
    return (
        jnp.concatenate([jnp.cos(angles), jnp.cos(angles)], axis=1),
        jnp.concatenate([jnp.sin(angles), jnp.sin(angles)], axis=1),
    )


def rotate(values, cosine, sine_table):
    half_dim = values.shape[-1] // 2
    turned = jnp.concatenate([-values[..., half_dim:], values[..., :half_dim]], axis=-1)
    return values * cosine[:, None, :] + turned * sine_table[:, None, :]


def unrotate(grad_values, cosine, sine_table):
    half_dim = grad_values.shape[-1] // 2
    scaled = grad_values * sine_table[:, None, :]
    turned = jnp.concatenate([scaled[..., half_dim:], -scaled[..., :half_dim]], axis=-1)
    return grad_values * cosine[:, None, :] + turned


def norm_backward(grad_hat, normed, inverse):
    return inverse * (grad_hat - normed * jnp.mean(grad_hat * normed, axis=-1, keepdims=True))


def token_places(seg_row, first_index, tok_count):
    own_segments = lax.dynamic_slice_in_dim(seg_row, first_index, tok_count, 0)
    doc_starts = jnp.sum((seg_row[None, :] < own_segments[:, None]).astype(jnp.int32), axis=1)
    positions = first_index + jnp.arange(tok_count, dtype=jnp.int32)
    return (positions - doc_starts).astype(single_precision)


def visible(seg_row, first_index, block_len):
    query_place = first_index + jnp.arange(block_len, dtype=jnp.int32)
    key_place = jnp.arange(seg_row.shape[0], dtype=jnp.int32)
    query_seg = lax.dynamic_slice_in_dim(seg_row, first_index, block_len, 0)
    return (key_place[None, :] <= query_place[:, None]) & (seg_row[None, :] == query_seg[:, None])


def attend(query_heads, key_heads, value_head_rows, seg_row, block_len):
    sequence_length = query_heads.shape[0]
    score_scale = HEAD_DIMENSION ** (-0.5)

    def one_block(block_index):
        first_index = block_index * block_len
        query_block = lax.dynamic_slice_in_dim(query_heads, first_index, block_len, 0)
        scores = (
            jnp.einsum(
                "qhd,khd->hqk", query_block, key_heads, preferred_element_type=single_precision
            )
            * score_scale
        )
        allowed = visible(seg_row, first_index, block_len)
        scores = jnp.where(allowed[None], scores, -1e30)
        row_top = jnp.max(scores, axis=2, keepdims=True)
        log_total = row_top + jnp.log(jnp.sum(jnp.exp(scores - row_top), axis=2, keepdims=True))
        prob_block = jnp.exp(scores - log_total).astype(reduced_precision)
        attended = jnp.einsum(
            "hqk,khd->qhd", prob_block, value_head_rows, preferred_element_type=single_precision
        )
        return (attended.astype(reduced_precision), log_total[:, :, 0])

    attended_all, log_totals = lax.map(
        one_block, jnp.arange(sequence_length // block_len, dtype=jnp.int32)
    )
    return (attended_all.reshape(query_heads.shape), log_totals)


def attend_back(
    query_heads, key_heads, value_head_rows, attended, out_grads, log_totals, seg_row, block_len
):
    sequence_length = query_heads.shape[0]
    score_scale = HEAD_DIMENSION ** (-0.5)

    def one_block(state_pair, inputs):
        key_grads, value_grads = state_pair
        block_index, log_total = inputs
        first_index = block_index * block_len
        query_block = lax.dynamic_slice_in_dim(query_heads, first_index, block_len, 0)
        out_block = lax.dynamic_slice_in_dim(attended, first_index, block_len, 0)
        grad_block = lax.dynamic_slice_in_dim(out_grads, first_index, block_len, 0)
        scores = (
            jnp.einsum(
                "qhd,khd->hqk", query_block, key_heads, preferred_element_type=single_precision
            )
            * score_scale
        )
        allowed = visible(seg_row, first_index, block_len)
        prob_block = jnp.where(allowed[None], jnp.exp(scores - log_total[:, :, None]), 0.0)
        rounded = prob_block.astype(reduced_precision)
        value_grads = value_grads + jnp.einsum(
            "hqk,qhd->khd", rounded, grad_block, preferred_element_type=single_precision
        )
        prob_grads = jnp.einsum(
            "qhd,khd->hqk", grad_block, value_head_rows, preferred_element_type=single_precision
        )
        row_delta = jnp.transpose(
            jnp.sum(
                grad_block.astype(single_precision) * out_block.astype(single_precision), axis=2
            )
        )
        score_grads = (prob_block * (prob_grads - row_delta[:, :, None]) * score_scale).astype(
            reduced_precision
        )
        query_grads = jnp.einsum(
            "hqk,khd->qhd", score_grads, key_heads, preferred_element_type=single_precision
        )
        key_grads = key_grads + jnp.einsum(
            "hqk,qhd->khd", score_grads, query_block, preferred_element_type=single_precision
        )
        return ((key_grads, value_grads), query_grads.astype(reduced_precision))

    zero_grads = jnp.zeros(query_heads.shape, single_precision)
    blocks = jnp.arange(sequence_length // block_len, dtype=jnp.int32)
    (key_grads, value_grads), query_all = lax.scan(
        one_block, (zero_grads, zero_grads), (blocks, log_totals)
    )
    return (
        query_all.reshape(query_heads.shape),
        key_grads.astype(reduced_precision),
        value_grads.astype(reduced_precision),
    )


def reduce_grads(left_parts, right_parts, owners, gain_block):
    group_size = lax.axis_size("sp")
    model_width = left_parts[0].shape[1]
    widths = [piece.shape[1] // group_size for piece in right_parts]
    packed = jnp.concatenate(
        [
            piece.reshape(piece.shape[0], group_size, width)
            for piece, width in zip(right_parts, widths)
        ],
        axis=2,
    )
    column_side = lax.all_to_all(packed, "sp", split_axis=1, concat_axis=0, tiled=True)
    column_side = column_side.reshape(column_side.shape[0], column_side.shape[2])
    left_joined = left_parts[0] if len(left_parts) == 1 else jnp.concatenate(left_parts, axis=1)
    left_all = lax.all_gather(left_joined, "sp", axis=0, tiled=True)
    partials = []
    offset = 0
    for owner, width in zip(owners, widths):
        left_piece = left_all[:, owner * model_width : (owner + 1) * model_width]
        partials.append(contract_first(left_piece, column_side[:, offset : offset + width]))
        offset = offset + width
    if gain_block is not None:
        partials.append(gain_block)
    summed = lax.psum_scatter(
        jnp.concatenate(partials, axis=1).astype(jnp.bfloat16),
        "fsdp",
        scatter_dimension=0,
        tiled=True,
    ).astype(jnp.float32)
    total_width = summed.shape[1]
    spread = lax.all_gather(summed.astype(jnp.bfloat16), "sp", axis=1, tiled=True).astype(
        summed.dtype
    )
    spread = spread.reshape(spread.shape[0], group_size, total_width)
    results = []
    offset = 0
    for width in widths:
        results.append(
            spread[:, :, offset : offset + width].reshape(spread.shape[0], group_size * width)
        )
        offset = offset + width
    if gain_block is not None:
        results.append(jnp.sum(spread[:, :, offset : offset + gain_block.shape[1]], axis=1))
    return results


def on_device(
    tokens,
    segments,
    prenorm,
    query_proj,
    key_projection,
    value_projection,
    query_norm,
    key_norm_gain,
    output_proj,
    postnorm,
    gate_proj,
    up_proj,
    down_proj,
    out_grad,
):
    token_rows = tokens.shape[0]
    model_width = tokens.shape[1]
    group_size = lax.axis_size("sp")
    fsdp_size = lax.axis_size("fsdp")
    seg_row = segments[0]
    sequence_length = seg_row.shape[0]
    block_len = min(512, sequence_length)
    head_repeat_factor = QUERY_HEADS // KEY_VALUE_HEADS
    local_heads = QUERY_HEADS // group_size
    places = token_places(seg_row, lax.axis_index("sp") * token_rows, token_rows)
    cosine, sine_table = rope_tables(places)
    tok_val = tokens.astype(single_precision)
    inv_one = lax.rsqrt(jnp.mean(tok_val * tok_val, axis=1, keepdims=True) + epsilon)
    hat_one = tok_val * inv_one
    gain_piece = lax.all_gather(prenorm, "fsdp", axis=0, tiled=True)
    query_piece = lax.all_gather(query_proj, "fsdp", axis=0, tiled=True)
    key_piece = lax.all_gather(key_projection, "fsdp", axis=0, tiled=True)
    value_piece = lax.all_gather(value_projection, "fsdp", axis=0, tiled=True)
    output_piece = lax.all_gather(output_proj, "fsdp", axis=0, tiled=True)
    columns = hat_one * gain_piece.astype(single_precision)[None, :]
    columns = columns.astype(reduced_precision)
    query_raw = jnp.dot(columns, query_piece, preferred_element_type=single_precision)
    key_unnormalized = jnp.dot(columns, key_piece, preferred_element_type=single_precision)
    value_unprojected = jnp.dot(columns, value_piece, preferred_element_type=single_precision)
    first_norm = columns
    prenorm_full = gain_piece
    query_raw = query_raw.reshape(token_rows, QUERY_HEADS, HEAD_DIMENSION)
    query_inv = lax.rsqrt(jnp.mean(query_raw * query_raw, axis=2, keepdims=True) + epsilon)
    query_hat = query_raw * query_inv
    query_rot = rotate(query_hat * query_norm.astype(single_precision), cosine, sine_table).astype(
        reduced_precision
    )
    key_unnormalized = key_unnormalized.reshape(token_rows, KEY_VALUE_HEADS, HEAD_DIMENSION)
    key_inverse_norm = lax.rsqrt(
        jnp.mean(key_unnormalized * key_unnormalized, axis=2, keepdims=True) + epsilon
    )
    key_normalized = key_unnormalized * key_inverse_norm
    key_rot = rotate(
        key_normalized * key_norm_gain.astype(single_precision), cosine, sine_table
    ).astype(reduced_precision)
    value_head_rows = value_unprojected.astype(reduced_precision).reshape(
        token_rows, KEY_VALUE_HEADS, HEAD_DIMENSION
    )
    stacked = jnp.stack(
        [
            query_rot.reshape(token_rows, QUERY_HEADS * HEAD_DIMENSION),
            jnp.repeat(key_rot, head_repeat_factor, axis=1).reshape(
                token_rows, QUERY_HEADS * HEAD_DIMENSION
            ),
            jnp.repeat(value_head_rows, head_repeat_factor, axis=1).reshape(
                token_rows, QUERY_HEADS * HEAD_DIMENSION
            ),
        ],
        axis=1,
    )
    by_heads = lax.all_to_all(stacked, "sp", split_axis=2, concat_axis=0, tiled=True)
    query_heads = by_heads[:, 0].reshape(sequence_length, local_heads, HEAD_DIMENSION)
    key_heads = by_heads[:, 1].reshape(sequence_length, local_heads, HEAD_DIMENSION)
    value_all = by_heads[:, 2].reshape(sequence_length, local_heads, HEAD_DIMENSION)
    attended, log_totals = attend(query_heads, key_heads, value_all, seg_row, block_len)
    attn_flat = lax.all_to_all(
        attended.reshape(sequence_length, local_heads * HEAD_DIMENSION),
        "sp",
        split_axis=0,
        concat_axis=1,
        tiled=True,
    )
    middle = tok_val + jnp.dot(attn_flat, output_piece, preferred_element_type=single_precision)
    inv_two = lax.rsqrt(jnp.mean(middle * middle, axis=1, keepdims=True) + epsilon)
    hat_two = middle * inv_two
    gain_piece = lax.all_gather(postnorm, "fsdp", axis=0, tiled=True)
    gate_piece = lax.all_gather(gate_proj, "fsdp", axis=0, tiled=True)
    up_piece = lax.all_gather(up_proj, "fsdp", axis=0, tiled=True)
    down_piece = lax.all_gather(down_proj, "fsdp", axis=0, tiled=True)
    columns = hat_two * gain_piece.astype(single_precision)[None, :]
    columns = columns.astype(reduced_precision)
    gate_val = jnp.dot(columns, gate_piece, preferred_element_type=single_precision)
    up_val = jnp.dot(columns, up_piece, preferred_element_type=single_precision)
    sigmoid_val = jax.nn.sigmoid(gate_val)
    silu_val = gate_val * sigmoid_val
    hidden = (silu_val * up_val).astype(reduced_precision)
    block_out = (middle + contract_last(hidden, down_piece)).astype(reduced_precision)
    hidden_grad = jnp.dot(out_grad, down_piece, preferred_element_type=single_precision)
    gate_grad = (
        hidden_grad * up_val * (sigmoid_val * (1.0 + gate_val * (1.0 - sigmoid_val)))
    ).astype(reduced_precision)
    up_grads = (hidden_grad * silu_val).astype(reduced_precision)
    norm_two_grad = contract_last(gate_grad, gate_piece) + contract_last(up_grads, up_piece)
    postnorm_part = jnp.sum(norm_two_grad * hat_two, axis=0)
    middle_grad = out_grad.astype(single_precision) + norm_backward(
        norm_two_grad * gain_piece.astype(single_precision), hat_two, inv_two
    )
    middle_half = middle_grad.astype(reduced_precision)
    grad_gate, grad_up, grad_down, grad_output = reduce_grads(
        [columns, out_grad, attn_flat],
        [gate_grad, up_grads, hidden, middle_half],
        [0, 0, 1, 2],
        None,
    )
    attn_grad = contract_last(middle_half, output_piece).astype(reduced_precision)
    grad_heads = lax.all_to_all(attn_grad, "sp", split_axis=1, concat_axis=0, tiled=True).reshape(
        sequence_length, local_heads, HEAD_DIMENSION
    )
    query_back, key_backward_pass, value_backward_pass = attend_back(
        query_heads, key_heads, value_all, attended, grad_heads, log_totals, seg_row, block_len
    )
    back_stack = jnp.stack(
        [
            query_back.reshape(sequence_length, local_heads * HEAD_DIMENSION),
            key_backward_pass.reshape(sequence_length, local_heads * HEAD_DIMENSION),
            value_backward_pass.reshape(sequence_length, local_heads * HEAD_DIMENSION),
        ],
        axis=1,
    )
    tokens_backward = lax.all_to_all(back_stack, "sp", split_axis=0, concat_axis=2, tiled=True)
    query_turn = unrotate(
        tokens_backward[:, 0]
        .astype(single_precision)
        .reshape(token_rows, QUERY_HEADS, HEAD_DIMENSION),
        cosine,
        sine_table,
    )
    key_gradient_sum = jnp.sum(
        tokens_backward[:, 1]
        .astype(single_precision)
        .reshape(token_rows, KEY_VALUE_HEADS, head_repeat_factor, HEAD_DIMENSION),
        axis=2,
    )
    value_gradient_sum = jnp.sum(
        tokens_backward[:, 2]
        .astype(single_precision)
        .reshape(token_rows, KEY_VALUE_HEADS, head_repeat_factor, HEAD_DIMENSION),
        axis=2,
    )
    key_rotated = unrotate(key_gradient_sum, cosine, sine_table)
    querynorm_part = jnp.sum(query_turn * query_hat, axis=(0, 1))
    keynorm_part = jnp.sum(key_rotated * key_normalized, axis=(0, 1))
    query_lin = (
        norm_backward(query_turn * query_norm.astype(single_precision), query_hat, query_inv)
        .reshape(token_rows, QUERY_HEADS * HEAD_DIMENSION)
        .astype(reduced_precision)
    )
    key_linear = (
        norm_backward(
            key_rotated * key_norm_gain.astype(single_precision), key_normalized, key_inverse_norm
        )
        .reshape(token_rows, KEY_VALUE_HEADS * HEAD_DIMENSION)
        .astype(reduced_precision)
    )
    value_linear = value_gradient_sum.reshape(token_rows, KEY_VALUE_HEADS * HEAD_DIMENSION).astype(
        reduced_precision
    )
    norm_one_grad = (
        contract_last(query_lin, query_piece)
        + contract_last(key_linear, key_piece)
        + contract_last(value_linear, value_piece)
    )
    prenorm_part = jnp.sum(norm_one_grad * hat_one, axis=0)
    input_grad = (
        middle_grad
        + norm_backward(norm_one_grad * prenorm_full.astype(single_precision), hat_one, inv_one)
    ).astype(reduced_precision)
    row_block = model_width // fsdp_size
    querynorm_tiled = jnp.tile(jnp.pad(querynorm_part, (0, row_block - HEAD_DIMENSION)), fsdp_size)
    keynorm_tiled = jnp.tile(jnp.pad(keynorm_part, (0, row_block - HEAD_DIMENSION)), fsdp_size)
    gain_block = jnp.stack([prenorm_part, postnorm_part, querynorm_tiled, keynorm_tiled], axis=1)
    grad_query, grad_key, grad_value, grad_gains = reduce_grads(
        [first_norm], [query_lin, key_linear, value_linear], [0, 0, 0], gain_block
    )
    return (
        block_out,
        input_grad,
        grad_gains[:, 0],
        grad_query,
        grad_key,
        grad_value,
        grad_gains[:HEAD_DIMENSION, 2],
        grad_gains[:HEAD_DIMENSION, 3],
        grad_output,
        grad_gains[:, 1],
        grad_gate,
        grad_up,
        grad_down,
    )


def solution(mesh):
    placed = (
        P(("fsdp", "sp"), None),
        P("fsdp", None),
        P("fsdp"),
        P("fsdp", None),
        P("fsdp", None),
        P("fsdp", None),
        P(),
        P(),
        P("fsdp", None),
        P("fsdp"),
        P("fsdp", None),
        P("fsdp", None),
        P("fsdp", None),
        P(("fsdp", "sp"), None),
    )
    return jax.shard_map(
        on_device,
        mesh=mesh,
        in_specs=placed,
        out_specs=(
            P(("fsdp", "sp"), None),
            P(("fsdp", "sp"), None),
            P("fsdp"),
            P("fsdp", None),
            P("fsdp", None),
            P("fsdp", None),
            P(),
            P(),
            P("fsdp", None),
            P("fsdp"),
            P("fsdp", None),
            P("fsdp", None),
            P("fsdp", None),
        ),
        check_vma=False,
    )
```

profile of v0, /device:TPU:0, one launch (start us, length us, event | category | flops | bytes accessed | tf_op | source)
XLA Modules:
  0.0 2450.9 jit_solution(6305920694864874208)
XLA Ops:
  27.0 66.1 %all-gather.19.cloned.1.call-done = bf16[2048,1024]{1,0:T(8,128)(2,1)} async-done(((bf16[512,1024]{1,0:T(8,128)(2,1)}), bf16[2048,1024]{1,0:T(8,128)(2,1)}) %all-gather.19.cloned.1.call-update) | async-done | bytes 4194320 | tf_op jit(solution)/shard_map/all_gather | solution.py:236
  96.8 77.1 %all-gather.17.cloned.1.call-done = bf16[2048,1024]{1,0:T(8,128)(2,1)} async-done(((bf16[512,1024]{1,0:T(8,128)(2,1)}), bf16[2048,1024]{1,0:T(8,128)(2,1)}) %all-gather.17.cloned.1.call-update) | async-done | bytes 4194320 | tf_op jit(solution)/shard_map/all_gather | solution.py:235
  178.9 144.7 %all-gather.15.cloned.1.call-done = bf16[2048,2048]{1,0:T(8,128)(2,1)} async-done(((bf16[512,2048]{1,0:T(8,128)(2,1)}), bf16[2048,2048]{1,0:T(8,128)(2,1)}) %all-gather.15.cloned.1.call-update) | async-done | bytes 8388624 | tf_op jit(solution)/shard_map/all_gather | solution.py:234
  340.5 25.9 %all-to-all-done = bf16[128,3,2048]{0,1,2:T(4,128)(2,1)} async-done(((bf16[128,3,2048]{0,1,2:T(4,128)(2,1)}), bf16[128,3,2048]{0,1,2:T(4,128)(2,1)}, u32[]{:S(2)}, u32[]{:S(2)}) %all-to-all-start) | async-done | bytes 1572896 | tf_op jit(solution)/shard_map/all_to_all | solution.py:274
  390.5 16.9 all-gather.1
  407.5 65.5 %all-gather.21.cloned.1.call-done = bf16[2048,2048]{1,0:T(8,128)(2,1)} async-done(((bf16[512,2048]{1,0:T(8,128)(2,1)}), bf16[2048,2048]{1,0:T(8,128)(2,1)}) %all-gather.21.cloned.1.call-update) | async-done | bytes 8388624 | tf_op jit(solution)/shard_map/all_gather | solution.py:237
  479.4 418.5 %all-gather.23.cloned.1.call-done = bf16[2048,6144]{1,0:T(8,128)(2,1)} async-done(((bf16[512,6144]{1,0:T(8,128)(2,1)}), bf16[2048,6144]{1,0:T(8,128)(2,1)}) %all-gather.23.cloned.1.call-update) | async-done | bytes 25165840 | tf_op jit(solution)/shard_map/all_gather | solution.py:290
  897.8 14.8 fusion.106
  912.6 410.0 %all-gather.25.cloned.1.call-done = bf16[2048,6144]{1,0:T(8,128)(2,1)} async-done(((bf16[512,6144]{1,0:T(8,128)(2,1)}), bf16[2048,6144]{1,0:T(8,128)(2,1)}) %all-gather.25.cloned.1.call-update) | async-done | bytes 25165840 | tf_op jit(solution)/shard_map/all_gather | solution.py:291
  1322.6 14.6 fusion.107
  1337.2 410.3 %all-gather.27.cloned.1.call-done = bf16[2048,6144]{1,0:T(8,128)(2,1)} async-done(((bf16[512,6144]{1,0:T(8,128)(2,1)}), bf16[2048,6144]{1,0:T(8,128)(2,1)}) %all-gather.27.cloned.1.call-update) | async-done | bytes 25165840 | tf_op jit(solution)/shard_map/all_gather | solution.py:292
  1747.6 15.5 multiply_convert_fusion.1
  1763.1 14.3 fusion.108
  1777.5 14.0 multiply_reduce_fusion.1
  1807.3 14.0 all-to-all-done.2
  1822.6 38.2 %while.28 = (s32[]{:T(128)}, f32[1024,2,128]{0,2,1:T(8,128)}, f32[1024,2,128]{0,2,1:T(8,128)}, bf16[2,512,2,128]{3,2,1,0:T(2,128)(2,1)}, s32[2]{0:T(128)S(1)}, /...) while((s32[]{:T(128)}, f32[1024,2,128]{0,2,1:T(8,128)}, ...), condition=%wide.region_12.13_spmd.clone, body=%wide.region_10.12_spmd.clone.sunk | while | flops 1356987904 | bytes 52730232 | solution.py:147
  1871.3 26.5 %all-to-all-done.3 = bf16[1024,3,256]{2,1,0:T(4,128)(2,1)S(1)} async-done(((bf16[1024,3,256]{2,1,0:T(4,128)(2,1)}), bf16[1024,3,256]{2,1,0:T(4,128)(2,1)S(1)}, u32[]{:S(2)}, u32[]{:S(2)}) %all-to-all-start.3) | async-done | bytes 1572896 | tf_op jit(solution)/shard_map/all_to_all | solution.py:333
  1977.1 28.0 %all-to-all-done.5 = bf16[128,8,2560]{2,0,1:T(8,128)(2,1)} async-done(((bf16[128,8,2560]{2,0,1:T(8,128)(2,1)}), bf16[128,8,2560]{2,0,1:T(8,128)(2,1)}, u32[]{:S(2)}, u32[]{:S(2)}) %all-to-all-start.5) | async-done | bytes 5242912 | tf_op jit(solution)/shard_map/all_to_all | solution.py:168
  2025.7 28.4 %pad_maximum_fusion = bf16[2048,2560]{0,1:T(8,128)(2,1)} fusion(bf16[2048,256]{0,1:T(8,128)(2,1)S(1)} %fusion.53, bf16[2048,768]{0,1:T(8,128)(2,1)S(1)} %fusion.49, bf16[2048,768]{0,1:T(8,128)(2,1)S(1)} %fusion.46, bf16[2048,768]{0,1:T(8,128)(2,1)S(1)} %fusion.43), kind=kLoop, calls=%fused_computation.47 | loop fusion | flops 41943040 | bytes 20971520 | tf_op jit(solution)/shard_map/concatenate | solution.py:181
  2054.8 174.4 %reduce-scatter.5.cloned.1.call-done = bf16[512,2560]{0,1:T(8,128)(2,1)} async-done(((bf16[2048,2560]{0,1:T(8,128)(2,1)}), bf16[512,2560]{0,1:T(8,128)(2,1)}) %reduce-scatter.5.cloned.1.call-update) | async-done | bytes 2621456 | tf_op jit(solution)/shard_map/reduce_scatter | solution.py:180
  2229.3 14.3 fusion.56
  2246.6 22.3 all-gather.35.cloned.1.call-done
  2303.9 74.4 %all-gather.33.cloned.1.call-done = bf16[512,20480]{0,1:T(8,128)(2,1)} async-done(((bf16[512,2560]{0,1:T(8,128)(2,1)}), bf16[512,20480]{0,1:T(8,128)(2,1)}) %all-gather.33.cloned.1.call-update) | async-done | bytes 20971536 | tf_op jit(solution)/shard_map/all_gather | solution.py:187
  2382.5 18.3 fusion.97
  (384 shorter events, 333.6 us)
Async XLA Ops:
  7.2 85.9 %all-gather.19.cloned.1.call-start = ((), (), s32[]{:S(2)}) async-start(), calls=%async_computation.10 | async-start | bytes 5242880 | tf_op jit(solution)/shard_map/all_gather | solution.py:236
  7.9 166.0 %all-gather.17.cloned.1.call-start = ((), (), s32[]{:S(2)}) async-start(), calls=%async_computation.9 | async-start | bytes 5242880 | tf_op jit(solution)/shard_map/all_gather | solution.py:235
  8.7 314.9 %all-gather.15.cloned.1.call-start = ((), (), s32[]{:S(2)}) async-start(), calls=%async_computation.8 | async-start | bytes 10485760 | tf_op jit(solution)/shard_map/all_gather | solution.py:234
  9.4 463.6 %all-gather.21.cloned.1.call-start = ((), (), s32[]{:S(2)}) async-start(), calls=%async_computation.11 | async-start | bytes 10485760 | tf_op jit(solution)/shard_map/all_gather | solution.py:237
  10.0 887.8 %all-gather.23.cloned.1.call-start = ((), (), s32[]{:S(2)}) async-start(), calls=%async_computation.12 | async-start | bytes 31457280 | tf_op jit(solution)/shard_map/all_gather | solution.py:290
  10.6 1312.1 %all-gather.25.cloned.1.call-start = ((), (), s32[]{:S(2)}) async-start(), calls=%async_computation.13 | async-start | bytes 31457280 | tf_op jit(solution)/shard_map/all_gather | solution.py:291
  11.2 1736.4 %all-gather.27.cloned.1.call-start = ((), (), s32[]{:S(2)}) async-start(), calls=%async_computation.14 | async-start | bytes 31457280 | tf_op jit(solution)/shard_map/all_gather | solution.py:292
  26.5 303.8 %copy-start.42 = (f32[128,128]{1,0:T(8,128)}, f32[128,128]{1,0:T(8,128)S(1)}, u32[]{:S(2)}) copy-start(f32[128,128]{1,0:T(8,128)S(1)} %get-tuple-element.443) | copy-start | bytes 196612
  26.5 304.2 %copy-start.38 = (f32[128,128]{1,0:T(8,128)}, f32[128,128]{1,0:T(8,128)S(1)}, u32[]{:S(2)}) copy-start(f32[128,128]{1,0:T(8,128)S(1)} %get-tuple-element.442) | copy-start | bytes 196612
  26.7 304.4 %copy-start.54 = (f32[2048]{0:T(1024)}, f32[2048]{0:T(1024)S(1)}, u32[]{:S(2)}) copy-start(f32[2048]{0:T(1024)S(1)} %broadcast_bitcast_fusion) | copy-start | bytes 24580
  335.4 31.0 %all-to-all-start = ((bf16[128,3,2048]{0,1,2:T(4,128)(2,1)}), bf16[128,3,2048]{0,1,2:T(4,128)(2,1)}, u32[]{:S(2)}, u32[]{:S(2)}) async-start(bf16[128,3,2048]{0,1,2:T(4,128)(2,1)} %copy.188), calls=%async_computation | async-start | bytes 4194304 | tf_op jit(solution)/shard_map/all_to_all | solution.py:274
  339.8 1623.2 %all-gather.29.cloned.1.call-start = ((), (), s32[]{:S(2)}) async-start(), calls=%async_computation.15 | async-start | bytes 4718592 | tf_op jit(solution)/shard_map/all_gather | solution.py:171
  386.9 20.5 all-to-all-start.1
  390.4 1586.7 %all-gather.31.cloned.1.call-start = ((), (), s32[]{:S(2)}) async-start(), calls=%async_computation.17 | async-start | bytes 14155776 | tf_op jit(solution)/shard_map/all_gather | solution.py:171
  477.8 1313.7 %copy-start.1 = (f32[128,2048]{1,0:T(8,128)}, f32[128,2048]{1,0:T(8,128)S(1)}, u32[]{:S(2)}) copy-start(f32[128,2048]{1,0:T(8,128)S(1)} %get-tuple-element.439) | copy-start | bytes 3145732
  912.6 835.0 %copy-start.30 = (bf16[128,2048]{1,0:T(8,128)(2,1)S(1)}, bf16[128,2048]{1,0:T(8,128)(2,1)}, u32[]{:S(2)}) copy-start(bf16[128,2048]{1,0:T(8,128)(2,1)} %param.31) | copy-start | bytes 1572868
  1802.4 18.8 all-to-all-start.2
  1867.3 30.6 %all-to-all-start.3 = ((bf16[1024,3,256]{2,1,0:T(4,128)(2,1)}), bf16[1024,3,256]{2,1,0:T(4,128)(2,1)S(1)}, u32[]{:S(2)}, u32[]{:S(2)}) async-start(bf16[1024,3,256]{2,1,0:T(4,128)(2,1)} %copy.209), calls=%async_computation.3 | async-start | bytes 4194304 | tf_op jit(solution)/shard_map/all_to_all | solution.py:333
  1920.4 19.7 all-to-all-start.4
  1940.0 65.2 %all-to-all-start.5 = ((bf16[128,8,2560]{2,0,1:T(8,128)(2,1)}), bf16[128,8,2560]{2,0,1:T(8,128)(2,1)}, u32[]{:S(2)}, u32[]{:S(2)}) async-start(bf16[128,8,2560]{2,0,1:T(8,128)(2,1)} %pad_maximum_fusion.1), calls=%async_computation.6 | async-start | bytes 10485760 | tf_op jit(solution)/shard_map/all_to_all | solution.py:168
  1944.8 109.4 %reduce-scatter.3.cloned.1.call-start = ((), (), s32[]{:S(2)}) async-start(), calls=%async_computation.16 | async-start | bytes 2662400 | tf_op jit(solution)/shard_map/reduce_scatter | solution.py:180
  1976.9 252.4 %reduce-scatter.5.cloned.1.call-start = ((), (), s32[]{:S(2)}) async-start(), calls=%async_computation.18 | async-start | bytes 13107200 | tf_op jit(solution)/shard_map/reduce_scatter | solution.py:180
  2054.2 214.7 %all-gather.35.cloned.1.call-start = ((), (), s32[]{:S(2)}) async-start(), calls=%async_computation.20 | async-start | bytes 4792320 | tf_op jit(solution)/shard_map/all_gather | solution.py:187
  2054.8 323.5 %all-gather.33.cloned.1.call-start = ((), (), s32[]{:S(2)}) async-start(), calls=%async_computation.19 | async-start | bytes 23592960 | tf_op jit(solution)/shard_map/all_gather | solution.py:187
  (69 other events, 1616.6 us)
Sparse Core Ops, SparseCore 0:
  9.6 83.4 all-gather.18
  94.6 79.2 all-gather.16
  175.5 148.0 all-gather.14
  325.0 147.9 all-gather.20
  474.4 423.3 all-gather.22
  899.3 423.3 all-gather.24
  1324.2 423.3 all-gather.26
  1749.5 34.7 all-gather.28
  1786.7 77.6 all-gather.30
  1977.0 43.1 reduce-scatter.2
  2054.3 174.8 reduce-scatter.4
  2231.0 37.8 all-gather.34
  2270.8 107.4 all-gather.32
where the time goes:
time: 2460 us; the launch traced here: 2450 us
  waiting for transfers between devices  1970 us (80%)
  matrix products  179 us (7%)
  local copies, waits for them, and re-layouts  154 us (6%)
  other arithmetic  72.6 us (3%)
  blocking collectives  30.6 us (1%)
  starting transfers between devices  25.8 us (1%)
    all_gather x1, waiting for transfers between devices, on_device(): gate_piece = lax.all_gather(gate_proj, 'fsdp', axis=0, tiled=True)  418 us
    all_gather x1, waiting for transfers between devices, on_device(): down_piece = lax.all_gather(down_proj, 'fsdp', axis=0, tiled=True)  410 us
    all_gather x1, waiting for transfers between devices, on_device(): up_piece = lax.all_gather(up_proj, 'fsdp', axis=0, tiled=True)  410 us
    reduce_scatter x2, waiting for transfers between devices, reduce_grads(): lax.psum_scatter(jnp.concatenate(partials, axis=1).astype(jnp.bfloat16),...  174 us
    all_gather x1, waiting for transfers between devices, on_device(): query_piece = lax.all_gather(query_proj, 'fsdp', axis=0, tiled=True)  145 us
    all_gather x2, waiting for transfers between devices, reduce_grads(): lax.all_gather(summed.astype(jnp.bfloat16), 'sp', axis=1, tiled=True)  96.7 us
    all_gather x1, waiting for transfers between devices, on_device(): key_piece = lax.all_gather(key_projection, 'fsdp', axis=0, tiled=True)  77.1 us
    all_gather x1, waiting for transfers between devices, on_device(): value_piece = lax.all_gather(value_projection, 'fsdp', axis=0, tiled=True)  66.1 us
  transfers between devices with their start and end apart: 19, of which 15 were waited for; matrix products, arithmetic and copies ran while one was open for 13% of the time, Pallas kernels for 0%

commit v1 on v0

v1 whole, which is shorter than its diff:
```python
import jax
import jax.numpy as jnp
from jax import lax
from jax.sharding import PartitionSpec as P

QUERY_HEADS = 16
KEY_VALUE_HEADS = 8
HEAD_DIMENSION = 128


epsilon = 1e-06
rope_base = 1000000.0
single_precision = jnp.float32
reduced_precision = jnp.bfloat16


def contract_last(left_side, right_side):
    return lax.dot_general(
        left_side, right_side, (((1,), (1,)), ((), ())), preferred_element_type=single_precision
    )


def contract_first(left_side, right_side):
    return lax.dot_general(
        left_side, right_side, (((0,), (0,)), ((), ())), preferred_element_type=single_precision
    )


def rope_tables(places):
    half_dim = HEAD_DIMENSION // 2
    frequency = jnp.power(
        rope_base, -(jnp.arange(half_dim, dtype=single_precision) * (2.0 / HEAD_DIMENSION))
    )
    angles = places[:, None] * frequency[None, :]
    return (
        jnp.concatenate([jnp.cos(angles), jnp.cos(angles)], axis=1),
        jnp.concatenate([jnp.sin(angles), jnp.sin(angles)], axis=1),
    )


def rotate(values, cosine, sine_table):
    half_dim = values.shape[-1] // 2
    turned = jnp.concatenate([-values[..., half_dim:], values[..., :half_dim]], axis=-1)
    return values * cosine[:, None, :] + turned * sine_table[:, None, :]


def unrotate(grad_values, cosine, sine_table):
    half_dim = grad_values.shape[-1] // 2
    scaled = grad_values * sine_table[:, None, :]
    turned = jnp.concatenate([scaled[..., half_dim:], -scaled[..., :half_dim]], axis=-1)
    return grad_values * cosine[:, None, :] + turned


def norm_backward(grad_hat, normed, inverse):
    return inverse * (grad_hat - normed * jnp.mean(grad_hat * normed, axis=-1, keepdims=True))


def token_places(seg_row, first_index, tok_count):
    own_segments = lax.dynamic_slice_in_dim(seg_row, first_index, tok_count, 0)
    doc_starts = jnp.sum((seg_row[None, :] < own_segments[:, None]).astype(jnp.int32), axis=1)
    positions = first_index + jnp.arange(tok_count, dtype=jnp.int32)
    return (positions - doc_starts).astype(single_precision)


def visible(seg_row, first_index, block_len):
    query_place = first_index + jnp.arange(block_len, dtype=jnp.int32)
    key_place = jnp.arange(seg_row.shape[0], dtype=jnp.int32)
    query_seg = lax.dynamic_slice_in_dim(seg_row, first_index, block_len, 0)
    return (key_place[None, :] <= query_place[:, None]) & (seg_row[None, :] == query_seg[:, None])


def attend(query_heads, key_heads, value_head_rows, seg_row, block_len):
    sequence_length = query_heads.shape[0]
    score_scale = HEAD_DIMENSION ** (-0.5)

    def one_block(block_index):
        first_index = block_index * block_len
        query_block = lax.dynamic_slice_in_dim(query_heads, first_index, block_len, 0)
        scores = (
            jnp.einsum(
                "qhd,khd->hqk", query_block, key_heads, preferred_element_type=single_precision
            )
            * score_scale
        )
        allowed = visible(seg_row, first_index, block_len)
        scores = jnp.where(allowed[None], scores, -1e30)
        row_top = jnp.max(scores, axis=2, keepdims=True)
        log_total = row_top + jnp.log(jnp.sum(jnp.exp(scores - row_top), axis=2, keepdims=True))
        prob_block = jnp.exp(scores - log_total).astype(reduced_precision)
        attended = jnp.einsum(
            "hqk,khd->qhd", prob_block, value_head_rows, preferred_element_type=single_precision
        )
        return (attended.astype(reduced_precision), log_total[:, :, 0])

    attended_all, log_totals = lax.map(
        one_block, jnp.arange(sequence_length // block_len, dtype=jnp.int32)
    )
    return (attended_all.reshape(query_heads.shape), log_totals)


def attend_back(
    query_heads, key_heads, value_head_rows, attended, out_grads, log_totals, seg_row, block_len
):
    sequence_length = query_heads.shape[0]
    score_scale = HEAD_DIMENSION ** (-0.5)

    def one_block(state_pair, inputs):
        key_grads, value_grads = state_pair
        block_index, log_total = inputs
        first_index = block_index * block_len
        query_block = lax.dynamic_slice_in_dim(query_heads, first_index, block_len, 0)
        out_block = lax.dynamic_slice_in_dim(attended, first_index, block_len, 0)
        grad_block = lax.dynamic_slice_in_dim(out_grads, first_index, block_len, 0)
        scores = (
            jnp.einsum(
                "qhd,khd->hqk", query_block, key_heads, preferred_element_type=single_precision
            )
            * score_scale
        )
        allowed = visible(seg_row, first_index, block_len)
        prob_block = jnp.where(allowed[None], jnp.exp(scores - log_total[:, :, None]), 0.0)
        rounded = prob_block.astype(reduced_precision)
        value_grads = value_grads + jnp.einsum(
            "hqk,qhd->khd", rounded, grad_block, preferred_element_type=single_precision
        )
        prob_grads = jnp.einsum(
            "qhd,khd->hqk", grad_block, value_head_rows, preferred_element_type=single_precision
        )
        row_delta = jnp.transpose(
            jnp.sum(
                grad_block.astype(single_precision) * out_block.astype(single_precision), axis=2
            )
        )
        score_grads = (prob_block * (prob_grads - row_delta[:, :, None]) * score_scale).astype(
            reduced_precision
        )
        query_grads = jnp.einsum(
            "hqk,khd->qhd", score_grads, key_heads, preferred_element_type=single_precision
        )
        key_grads = key_grads + jnp.einsum(
            "hqk,qhd->khd", score_grads, query_block, preferred_element_type=single_precision
        )
        return ((key_grads, value_grads), query_grads.astype(reduced_precision))

    zero_grads = jnp.zeros(query_heads.shape, single_precision)
    blocks = jnp.arange(sequence_length // block_len, dtype=jnp.int32)
    (key_grads, value_grads), query_all = lax.scan(
        one_block, (zero_grads, zero_grads), (blocks, log_totals)
    )
    return (
        query_all.reshape(query_heads.shape),
        key_grads.astype(reduced_precision),
        value_grads.astype(reduced_precision),
    )


def plane_permute(piece, flip):
    size = lax.axis_size("sp")
    return lax.ppermute(piece, "sp", [(i, i ^ flip) for i in range(size)])


def plane_gather(piece):
    size = lax.axis_size("sp")
    if size != 8:
        return lax.all_gather(piece, "sp", axis=0)
    index = lax.axis_index("sp")
    chip, core = index // 2, index % 2
    found = [piece] + [plane_permute(piece, 2 * turn) for turn in (1, 2, 3)]
    mine = jnp.zeros((4,) + piece.shape, piece.dtype)
    for turn, part in enumerate(found):
        mine = lax.dynamic_update_index_in_dim(mine, part, chip ^ turn, 0)
    other = plane_permute(mine, 1)
    even = jnp.where(core == 0, mine, other)
    odd = jnp.where(core == 0, other, mine)
    return jnp.stack([even, odd], axis=1).reshape((8,) + piece.shape)


def plane_reduce(parts):
    size = lax.axis_size("sp")
    if size != 8:
        return lax.psum_scatter(parts, "sp", scatter_dimension=0, tiled=False).astype(
            single_precision
        )
    index = lax.axis_index("sp")
    chip, core = index // 2, index % 2
    split = parts.reshape((4, 2) + parts.shape[1:])
    given = lax.dynamic_index_in_dim(split, 1 - core, 1, keepdims=False)
    kept = lax.dynamic_index_in_dim(split, core, 1, keepdims=False)
    joined = (
        kept.astype(single_precision) + plane_permute(given, 1).astype(single_precision)
    ).astype(reduced_precision)
    total = lax.dynamic_index_in_dim(joined, chip, 0, keepdims=False).astype(single_precision)
    for turn in (1, 2, 3):
        sent = lax.dynamic_index_in_dim(joined, chip ^ turn, 0, keepdims=False)
        total = total + plane_permute(sent, 2 * turn).astype(single_precision)
    return total


def line_reduce(parts):
    size = lax.axis_size("fsdp")
    if size < 3:
        return lax.psum_scatter(parts, "fsdp", scatter_dimension=0, tiled=False)
    index = lax.axis_index("fsdp")

    def own(at):
        return lax.dynamic_index_in_dim(parts, at % size, 0, keepdims=False)

    def plus(left, right):
        return (left.astype(single_precision) + right.astype(single_precision)).astype(
            parts.dtype
        )

    first = own(jnp.where(index == 0, size - 1, 0))
    up = lax.ppermute(first, "fsdp", [(0, 1), (size - 1, size - 2)])
    down = up
    for step in range(2, size):
        up = lax.ppermute(
            plus(own(index + size - step), up), "fsdp", [(i, i + 1) for i in range(step)]
        )
        down = lax.ppermute(
            plus(own(index + step), down),
            "fsdp",
            [(i, i - 1) for i in range(size - step, size)],
        )
    return (
        own(index).astype(single_precision)
        + up.astype(single_precision)
        + down.astype(single_precision)
    ).astype(parts.dtype)


def columns_of(weight, first, width):
    return lax.dynamic_slice_in_dim(weight, first, width, 1)


def spread(reduced, widths):
    size = lax.axis_size("sp")
    everything = lax.all_gather(reduced, "sp", axis=0)
    rows = reduced.shape[0]
    results = []
    offset = 0
    for width in widths:
        piece = everything[:, :, offset : offset + width].astype(single_precision)
        results.append(jnp.transpose(piece, (1, 0, 2)).reshape(rows, size * width))
        offset = offset + width
    return results


def on_device(
    tokens,
    segments,
    prenorm,
    query_proj,
    key_projection,
    value_projection,
    query_norm,
    key_norm_gain,
    output_proj,
    postnorm,
    gate_proj,
    up_proj,
    down_proj,
    out_grad,
):
    token_rows, model_width = tokens.shape
    plane = lax.axis_size("sp")
    lines = lax.axis_size("fsdp")
    spot = lax.axis_index("sp")
    seg_row = segments[0]
    length = seg_row.shape[0]
    block_len = min(512, length)
    local_heads = QUERY_HEADS // plane
    query_width = local_heads * HEAD_DIMENSION
    share = max(1, plane // KEY_VALUE_HEADS)
    owned = HEAD_DIMENSION // share
    model_cols = model_width // plane
    ff_cols = gate_proj.shape[1] // plane
    row_block = model_width // lines

    everyone = plane_gather(tokens).reshape(length, model_width)
    gains = lax.all_gather(jnp.stack([prenorm, postnorm]), "fsdp", axis=1, tiled=True)
    prenorm_full = gains[0].astype(single_precision)
    postnorm_full = gains[1].astype(single_precision)
    kv_first = (spot // share) * HEAD_DIMENSION
    qkv_slice = jnp.concatenate(
        [
            columns_of(query_proj, spot * query_width, query_width),
            columns_of(key_projection, kv_first, HEAD_DIMENSION),
            columns_of(value_projection, kv_first, HEAD_DIMENSION),
        ],
        axis=1,
    )
    qkv = lax.all_gather(qkv_slice, "fsdp", axis=0, tiled=True)
    out_cols = lax.all_gather(
        columns_of(output_proj, spot * model_cols, model_cols), "fsdp", axis=0, tiled=True
    )
    gate_up = lax.all_gather(
        jnp.concatenate(
            [
                columns_of(gate_proj, spot * ff_cols, ff_cols),
                columns_of(up_proj, spot * ff_cols, ff_cols),
            ],
            axis=1,
        ),
        "fsdp",
        axis=0,
        tiled=True,
    )
    down_cols = lax.all_gather(
        columns_of(down_proj, spot * ff_cols, ff_cols), "fsdp", axis=0, tiled=True
    )

    places = token_places(seg_row, 0, length)
    cosine, sine_table = rope_tables(places)
    tok_val = everyone.astype(single_precision)
    inv_one = lax.rsqrt(jnp.mean(tok_val * tok_val, axis=1, keepdims=True) + epsilon)
    first_norm = (tok_val * inv_one * prenorm_full[None, :]).astype(reduced_precision)
    raw = jnp.dot(first_norm, qkv, preferred_element_type=single_precision)
    query_raw = raw[:, :query_width].reshape(length, local_heads, HEAD_DIMENSION)
    key_raw = raw[:, query_width : query_width + HEAD_DIMENSION].reshape(length, 1, HEAD_DIMENSION)
    value_one = raw[:, query_width + HEAD_DIMENSION :].astype(reduced_precision)
    query_inv = lax.rsqrt(jnp.mean(query_raw * query_raw, axis=2, keepdims=True) + epsilon)
    query_hat = query_raw * query_inv
    query_rot = rotate(query_hat * query_norm.astype(single_precision), cosine, sine_table).astype(
        reduced_precision
    )
    key_inv = lax.rsqrt(jnp.mean(key_raw * key_raw, axis=2, keepdims=True) + epsilon)
    key_hat = key_raw * key_inv
    key_rot = rotate(key_hat * key_norm_gain.astype(single_precision), cosine, sine_table).astype(
        reduced_precision
    )
    key_heads = jnp.repeat(key_rot, local_heads, axis=1)
    value_heads = jnp.repeat(value_one.reshape(length, 1, HEAD_DIMENSION), local_heads, axis=1)
    attended, log_totals = attend(query_rot, key_heads, value_heads, seg_row, block_len)
    attn_all = plane_gather(attended.reshape(length, query_width))
    attn_all = jnp.transpose(attn_all, (1, 0, 2)).reshape(length, model_width)
    middle_cols = columns_of(everyone, spot * model_cols, model_cols).astype(
        single_precision
    ) + jnp.dot(attn_all, out_cols, preferred_element_type=single_precision)
    middle_all = plane_gather(middle_cols.astype(reduced_precision))
    middle_all = jnp.transpose(middle_all, (1, 0, 2)).reshape(length, model_width)
    middle = middle_all.astype(single_precision)
    inv_two = lax.rsqrt(jnp.mean(middle * middle, axis=1, keepdims=True) + epsilon)
    second_norm = (middle * inv_two * postnorm_full[None, :]).astype(reduced_precision)
    middle_own = lax.dynamic_slice_in_dim(
        middle_all, spot * token_rows, token_rows, 0
    ).astype(single_precision)
    inv_two_own = lax.dynamic_slice_in_dim(inv_two, spot * token_rows, token_rows, 0)
    hat_two_own = middle_own * inv_two_own

    grads_all = plane_gather(out_grad).reshape(length, model_width)
    gate_up_val = jnp.dot(second_norm, gate_up, preferred_element_type=single_precision)
    gate_val = gate_up_val[:, :ff_cols]
    up_val = gate_up_val[:, ff_cols:]
    sigmoid_val = jax.nn.sigmoid(gate_val)
    silu_val = gate_val * sigmoid_val
    hidden = (silu_val * up_val).astype(reduced_precision)
    down_part = contract_first(grads_all, hidden).astype(reduced_precision)
    down_sum = line_reduce(down_part.reshape(lines, row_block, ff_cols))
    hidden_grad = jnp.dot(grads_all, down_cols, preferred_element_type=single_precision)
    gate_grad = (
        hidden_grad * up_val * (sigmoid_val * (1.0 + gate_val * (1.0 - sigmoid_val)))
    ).astype(reduced_precision)
    up_grads = (hidden_grad * silu_val).astype(reduced_precision)
    both_grads = jnp.concatenate([gate_grad, up_grads], axis=1)
    norm_two_part = contract_last(both_grads, gate_up).astype(reduced_precision)
    norm_two_grad = plane_reduce(norm_two_part.reshape(plane, token_rows, model_width))
    gate_up_part = contract_first(second_norm, both_grads).astype(reduced_precision)
    gate_up_sum = line_reduce(gate_up_part.reshape(lines, row_block, 2 * ff_cols))
    block_part = contract_last(hidden, down_cols).astype(reduced_precision)
    block_out = (
        middle_own + plane_reduce(block_part.reshape(plane, token_rows, model_width))
    ).astype(reduced_precision)

    postnorm_part = jnp.sum(norm_two_grad * hat_two_own, axis=0)
    middle_grad = out_grad.astype(single_precision) + norm_backward(
        norm_two_grad * postnorm_full, hat_two_own, inv_two_own
    )
    half_all = plane_gather(middle_grad.astype(reduced_precision)).reshape(length, model_width)
    out_part = contract_first(
        attn_all, columns_of(half_all, spot * model_cols, model_cols)
    ).astype(reduced_precision)
    out_rows = lax.all_to_all(
        out_cols.reshape(plane, query_width, model_cols), "sp", split_axis=0, concat_axis=0, tiled=True
    )
    out_rows = jnp.transpose(
        out_rows.reshape(plane, query_width, model_cols), (1, 0, 2)
    ).reshape(query_width, model_width)
    attn_grad = contract_last(half_all, out_rows).astype(reduced_precision)
    query_back, key_back, value_back = attend_back(
        query_rot,
        key_heads,
        value_heads,
        attended,
        attn_grad.reshape(length, local_heads, HEAD_DIMENSION),
        log_totals,
        seg_row,
        block_len,
    )
    query_turn = unrotate(query_back.astype(single_precision), cosine, sine_table)
    key_sum = jnp.sum(key_back.astype(single_precision), axis=1, keepdims=True)
    value_sum = jnp.sum(value_back.astype(single_precision), axis=1)
    if share > 1:
        groups = [
            [first + offset for offset in range(share)] for first in range(0, plane, share)
        ]
        both = jnp.concatenate([key_sum[:, 0], value_sum], axis=1)
        gathered = [both]
        for turn in range(1, share):
            pairs = [
                (group[i], group[(i + turn) % share]) for group in groups for i in range(share)
            ]
            gathered.append(lax.ppermute(both, "sp", pairs))
        both = sum(gathered[1:], gathered[0])
        key_sum = both[:, None, :HEAD_DIMENSION]
        value_sum = both[:, HEAD_DIMENSION:]
    key_turn = unrotate(key_sum, cosine, sine_table)
    querynorm_part = jnp.sum(query_turn * query_hat, axis=(0, 1))
    keynorm_part = jnp.sum(key_turn * key_hat, axis=(0, 1)) / share
    query_lin = (
        norm_backward(query_turn * query_norm.astype(single_precision), query_hat, query_inv)
        .reshape(length, query_width)
        .astype(reduced_precision)
    )
    key_lin = (
        norm_backward(key_turn * key_norm_gain.astype(single_precision), key_hat, key_inv)
        .reshape(length, HEAD_DIMENSION)
        .astype(reduced_precision)
    )
    value_lin = value_sum.astype(reduced_precision)
    if share > 1:
        own_first = (spot % share) * owned
        key_lin = columns_of(key_lin, own_first, owned)
        value_lin = columns_of(value_lin, own_first, owned)
        qkv = jnp.concatenate(
            [
                qkv[:, :query_width],
                columns_of(qkv, query_width + own_first, owned),
                columns_of(qkv, query_width + HEAD_DIMENSION + own_first, owned),
            ],
            axis=1,
        )
    lin = jnp.concatenate([query_lin, key_lin, value_lin], axis=1)
    norm_one_part = contract_last(lin, qkv).astype(reduced_precision)
    qkv_part = contract_first(first_norm, lin).astype(reduced_precision)
    attn_part = jnp.concatenate([qkv_part, out_part], axis=1)
    attn_sum = line_reduce(attn_part.reshape(lines, row_block, attn_part.shape[1]))
    norm_one_grad = plane_reduce(norm_one_part.reshape(plane, token_rows, model_width))
    own_tok = tokens.astype(single_precision)
    inv_own = lax.rsqrt(jnp.mean(own_tok * own_tok, axis=1, keepdims=True) + epsilon)
    hat_own = own_tok * inv_own
    prenorm_part = jnp.sum(norm_one_grad * hat_own, axis=0)
    input_grad = (
        middle_grad + norm_backward(norm_one_grad * prenorm_full, hat_own, inv_own)
    ).astype(reduced_precision)
    small = lax.psum(
        jnp.concatenate([prenorm_part, postnorm_part, querynorm_part, keynorm_part]),
        ("fsdp", "sp"),
    )
    row_first = lax.axis_index("fsdp") * row_block
    grad_prenorm = lax.dynamic_slice_in_dim(small, row_first, row_block, 0)
    grad_postnorm = lax.dynamic_slice_in_dim(small, model_width + row_first, row_block, 0)
    grad_querynorm = small[2 * model_width : 2 * model_width + HEAD_DIMENSION]
    grad_keynorm = small[2 * model_width + HEAD_DIMENSION :]
    (grad_down,) = spread(down_sum, [ff_cols])
    grad_gate, grad_up = spread(gate_up_sum, [ff_cols, ff_cols])
    grad_query, grad_key, grad_value, grad_output = spread(
        attn_sum, [query_width, owned, owned, model_cols]
    )
    return (
        block_out,
        input_grad,
        grad_prenorm,
        grad_query,
        grad_key,
        grad_value,
        grad_querynorm,
        grad_keynorm,
        grad_output,
        grad_postnorm,
        grad_gate,
        grad_up,
        grad_down,
    )


def solution(mesh):
    placed = (
        P(("fsdp", "sp"), None),
        P("fsdp", None),
        P("fsdp"),
        P("fsdp", None),
        P("fsdp", None),
        P("fsdp", None),
        P(),
        P(),
        P("fsdp", None),
        P("fsdp"),
        P("fsdp", None),
        P("fsdp", None),
        P("fsdp", None),
        P(("fsdp", "sp"), None),
    )
    return jax.shard_map(
        on_device,
        mesh=mesh,
        in_specs=placed,
        out_specs=(
            P(("fsdp", "sp"), None),
            P(("fsdp", "sp"), None),
            P("fsdp"),
            P("fsdp", None),
            P("fsdp", None),
            P("fsdp", None),
            P(),
            P(),
            P("fsdp", None),
            P("fsdp"),
            P("fsdp", None),
            P("fsdp", None),
            P("fsdp", None),
        ),
        check_vma=False,
    )
```

time: 2460 us -> 889 us (0.36)
  waiting for transfers between devices: 1970 us -> 328 us
  matrix products: 179 us -> 84.1 us
  blocking collectives: 30.6 us -> 91.2 us
  starting transfers between devices: 25.8 us -> 73 us
  other arithmetic: 72.6 us -> 105 us
    all_gather x11 -> x7, waiting for transfers between devices: 1690 us -> 38.3 us  [the longest x1 38.2 us: on_device(): lax.all_gather(columns_of(down_proj, spot * ff_cols, ff_cols), 'fsdp', ax...]
    ppermute x0 -> x47, waiting for transfers between devices: none -> 284 us  [the longest x32 138 us: plane_permute(): return lax.ppermute(piece, 'sp', [(i, i ^ flip) for i in range(size)])]
    reduce_scatter x2 -> x0, waiting for transfers between devices: 174 us -> none  [reduce_grads(): lax.psum_scatter(jnp.concatenate(partials, axis=1).astype(jnp.bfloat16),...]
    all_to_all x6 -> x1, waiting for transfers between devices: 101 us -> 5.55 us  [on_device(): lax.all_to_all(out_cols.reshape(plane, query_width, model_cols), 'sp', sp...]
    psum x0 -> x1, blocking collectives: none -> 77.8 us  [on_device(): lax.psum(jnp.concatenate([prenorm_part, postnorm_part, querynorm_part, ke...]
    ppermute x0 -> x47, starting transfers between devices: none -> 68.4 us  [the longest x32 28.9 us: plane_permute(): return lax.ppermute(piece, 'sp', [(i, i ^ flip) for i in range(size)])]
    unnamed x145 -> x126, local copies, waits for them, and re-layouts: 15.6 us -> 60.7 us
    dot_general x7 -> x4, matrix products: 60.7 us -> 17 us  [contract_last(): lax.dot_general(left_side, right_side, (((1,), (1,)), ((), ())), preferre...]
  transfers between devices with their start and end apart: 19 -> 55, of which waited for: 15 -> 28; matrix products, arithmetic and copies ran while one was open for 13% -> 31% of each run, Pallas kernels for 0% -> 0%
where the time goes in v1:
time: 889 us; the launch traced here: 877 us
  waiting for transfers between devices  328 us (37%)
  local copies, waits for them, and re-layouts  176 us (20%)
  other arithmetic  105 us (12%)
  blocking collectives  91.2 us (10%)
  matrix products  84.1 us (9%)
  starting transfers between devices  73 us (8%)
  between operations  15.9 us (2%)
    ppermute x32, waiting for transfers between devices, plane_permute(): return lax.ppermute(piece, 'sp', [(i, i ^ flip) for i in range(size)])  138 us
    ppermute x6, waiting for transfers between devices, line_reduce(): lax.ppermute(plus(own(index + size - step), up), 'fsdp', [(i, i + 1) for...  85.3 us
    psum x1, blocking collectives, on_device(): lax.psum(jnp.concatenate([prenorm_part, postnorm_part, querynorm_part, ke...  77.8 us
    unnamed x126, local copies, waits for them, and re-layouts  60.7 us
    ppermute x3, waiting for transfers between devices, line_reduce(): up = lax.ppermute(first, 'fsdp', [(0, 1), (size - 1, size - 2)])  46 us
    all_gather x1, waiting for transfers between devices, on_device(): lax.all_gather(columns_of(down_proj, spot * ff_cols, ff_cols), 'fsdp', ax...  38.2 us
    ppermute x32, starting transfers between devices, plane_permute(): return lax.ppermute(piece, 'sp', [(i, i ^ flip) for i in range(size)])  28.9 us
    ppermute x6, starting transfers between devices, line_reduce(): lax.ppermute(plus(own(index + size - step), up), 'fsdp', [(i, i + 1) for...  23.6 us
  transfers between devices with their start and end apart: 55, of which 28 were waited for; matrix products, arithmetic and copies ran while one was open for 31% of the time, Pallas kernels for 0%

profile of v1, /device:TPU:0, one launch (start us, length us, event | category | flops | bytes accessed | tf_op | source)
XLA Modules:
  0.0 876.7 jit_solution(7773381552337551677)
XLA Ops:
  17.4 11.5 %collective-permute-done = bf16[128,2048]{1,0:T(8,128)(2,1)} collective-permute-done((bf16[128,2048]{1,0:T(8,128)(2,1)}, bf16[128,2048]{1,0:T(8,128)(2,1)}, u32[]{:S(2)}, u32[]{:S(2)}) %collective-permute-start) | collective-permute-done | bytes 524320 | tf_op jit(solution)/shard_map/ppermute | solution.py:159
  43.4 13.5 %all_gather.33 = bf16[2,2048]{1,0:T(2,128)(2,1)S(1)} all-gather(bf16[2,512]{1,0:T(2,128)(2,1)S(1)} %pad_maximum_fusion.19), channel_id=1, replica_groups=mesh['fsdp'=4,'sp'=8] {'fsdp'}, dimensions={1}, use_global_device_ids=true | all-gather | bytes 10240 | tf_op jit(solution)/shard_map/all_gather | solution.py:281
  65.3 11.2 %copy.281 = bf16[4,2,128,2048]{2,1,0,3:T(2,128)(2,1)} copy(bf16[4,2,128,2048]{3,2,0,1:T(8,128)(2,1)} %pad_maximum_fusion) | data formatting | bytes 8388608 | tf_op jit(solution)/shard_map/stack | solution.py:175
  102.6 11.0 %while.28 = (s32[]{:T(128)}, bf16[2,512,2,128]{3,1,2,0:T(8,128)(2,1)S(1)}, f32[2,2,512]{2,1,0:T(2,128)S(1)}, s32[2]{0:T(128)S(1)}, s32[1,1024]{1,0:T(1,128)S(1)}...) while((s32[]{:T(128)}, ...), condition=%wide.region_7.8_spmd.clone, body=%wide.region_4.7_spmd.clone.sunk | while | flops 550108672 | bytes 16824560 | solution.py:95
  119.1 11.0 %collective-permute-done.4 = bf16[1024,256]{1,0:T(8,128)(2,1)} collective-permute-done((bf16[1024,256]{1,0:T(8,128)(2,1)}, bf16[1024,256]{1,0:T(8,128)(2,1)}, u32[]{:S(2)}, u32[]{:S(2)}) %collective-permute-start.4) | collective-permute-done | bytes 524320 | tf_op jit(solution)/shard_map/ppermute | solution.py:159
  155.5 12.3 %collective-permute-done.17 = bf16[128,2048]{1,0:T(8,128)(2,1)S(1)} collective-permute-done((bf16[128,2048]{1,0:T(8,128)(2,1)S(1)}, bf16[128,2048]{1,0:T(8,128)(2,1)S(1)}, u32[]{:S(2)}, u32[]{:S(2)}) %collective-permute-start.17) | collective-permute-done | bytes 524320 | tf_op jit(solution)/shard_map/ppermute | solution.py:159
  231.3 12.4 %fusion.75 = f32[1024,1536]{1,0:T(8,128)} fusion(bf16[2048,1536]{1,0:T(8,128)(2,1)} %all-gather.15.cloned.1.call-done, bf16[1024,2048]{1,0:T(8,128)(2,1)} %bitcast.375, f32[2048]{0:T(1024)S(1)} %bitcast.418, f32[1024]{0:T(1024)S(1)} %add_rsqrt_fusion.1), kind=kOutput, calls=%fused_computation.151 | convolution fusion | flops 6450839552 | bytes 16789504 | tf_op jit(solution)/shard_map/dot_general | solution.py:352
  243.7 38.2 %all-gather.17.cloned.1.call-done = bf16[2048,768]{1,0:T(8,128)(2,1)} async-done(((bf16[512,768]{1,0:T(8,128)(2,1)}), bf16[2048,768]{1,0:T(8,128)(2,1)}) %all-gather.17.cloned.1.call-update) | async-done | bytes 3145744 | tf_op jit(solution)/shard_map/all_gather | solution.py:309
  281.9 10.5 %multiply_convert_fusion.4 = (bf16[1024,768]{1,0:T(8,128)(2,1)S(1)}, bf16[1024,768]{1,0:T(8,128)(2,1)S(1)}, bf16[1024,768]{1,0:T(8,128)(2,1)}) fusion(f32[1024,1536]{1,0:T(8,128)} %fusion.75, bf16[1024,2048]{1,0:T(8,128)(2,1)} %bitcast.402, bf16[2048,768]{1,0:T(8,128)(2,1)} %all-gather.17.cloned.1.call-done), kind=kOutput, calls=%fused_computation.93 | convolution fusion | flops 3233021952 | bytes 18350080 | tf_op jit(solution)/shard_map/dot_general | solution.py:360
  325.6 11.4 %collective-permute-done.23 = bf16[128,2048]{1,0:T(8,128)(2,1)S(1)} collective-permute-done((bf16[128,2048]{1,0:T(8,128)(2,1)S(1)}, bf16[128,2048]{1,0:T(8,128)(2,1)S(1)}, u32[]{:S(2)}, u32[]{:S(2)}) %collective-permute-start.23) | collective-permute-done | bytes 524320 | tf_op jit(solution)/shard_map/ppermute | solution.py:159
  411.4 18.2 %while.29 = (s32[]{:T(128)}, f32[1024,2,128]{0,2,1:T(8,128)S(1)}, f32[1024,2,128]{0,2,1:T(8,128)}, bf16[2,512,2,128]{3,1,0,2:T(8,128)(2,1)S(1)}, s32[2]{0:T(128)...) while((s32[]{:T(128)}, f32[1024,2,128]{0,2,1:T(8,128)S(1)}, ...), condition=%wide.region_13.14_spmd.clone, body=%wide.region_11.13_spmd.clone.sunk | while | flops 1356987904 | bytes 37787996 | solution.py:147
  458.0 16.2 %collective-permute-done.32 = bf16[512,768]{1,0:T(8,128)(2,1)S(1)} collective-permute-done((bf16[512,768]{1,0:T(8,128)(2,1)S(1)}, bf16[512,768]{1,0:T(8,128)(2,1)S(1)}, u32[]{:S(2)}, u32[]{:S(2)}) %collective-permute-start.32) | collective-permute-done | bytes 786464 | tf_op jit(solution)/shard_map/ppermute | solution.py:214
  481.2 15.3 %collective-permute-done.33 = bf16[512,768]{1,0:T(8,128)(2,1)S(1)} collective-permute-done((bf16[512,768]{1,0:T(8,128)(2,1)S(1)}, bf16[512,768]{1,0:T(8,128)(2,1)S(1)}, u32[]{:S(2)}, u32[]{:S(2)}) %collective-permute-start.33) | collective-permute-done | bytes 786464 | tf_op jit(solution)/shard_map/ppermute | solution.py:217
  502.7 13.1 %collective-permute-done.34 = bf16[512,768]{1,0:T(8,128)(2,1)S(1)} collective-permute-done((bf16[512,768]{1,0:T(8,128)(2,1)S(1)}, bf16[512,768]{1,0:T(8,128)(2,1)S(1)}, u32[]{:S(2)}, u32[]{:S(2)}) %collective-permute-start.34) | collective-permute-done | bytes 786464 | tf_op jit(solution)/shard_map/ppermute | solution.py:217
  521.6 9.9 %convolution_convert_fusion.1 = bf16[2048,1536]{1,0:T(8,128)(2,1)S(1)} fusion(bf16[1024,768]{1,0:T(8,128)(2,1)} %copy-done.60, bf16[1024,768]{1,0:T(8,128)(2,1)} %copy-done.59, bf16[1024,2048]{1,0:T(8,128)(2,1)} %bitcast.378, f32[2048]{0:T(1024)S(1)} %bitcast.421, f32[1024]{0:T(1024)S(1)} %add_rsqrt_fusion.1), kind=kOutput, calls=%fused_computation.60 | convolution fusion | flops 6460276736 | bytes 13643776 | tf_op jit(solution)/shard_map/dot_general | solution.py:24
  535.4 29.8 %collective-permute-done.37 = bf16[512,1536]{1,0:T(8,128)(2,1)S(1)} collective-permute-done((bf16[512,1536]{1,0:T(8,128)(2,1)S(1)}, bf16[512,1536]{1,0:T(8,128)(2,1)S(1)}, u32[]{:S(2)}, u32[]{:S(2)}) %collective-permute-start.37) | collective-permute-done | bytes 1572896 | tf_op jit(solution)/shard_map/ppermute | solution.py:214
  571.4 29.1 %collective-permute-done.38 = bf16[512,1536]{1,0:T(8,128)(2,1)S(1)} collective-permute-done((bf16[512,1536]{1,0:T(8,128)(2,1)S(1)}, bf16[512,1536]{1,0:T(8,128)(2,1)S(1)}, u32[]{:S(2)}, u32[]{:S(2)}) %collective-permute-start.38) | collective-permute-done | bytes 1572896 | tf_op jit(solution)/shard_map/ppermute | solution.py:217
  607.5 26.8 %collective-permute-done.39 = bf16[512,1536]{1,0:T(8,128)(2,1)S(1)} collective-permute-done((bf16[512,1536]{1,0:T(8,128)(2,1)S(1)}, bf16[512,1536]{1,0:T(8,128)(2,1)S(1)}, u32[]{:S(2)}, u32[]{:S(2)}) %collective-permute-start.39) | collective-permute-done | bytes 1572896 | tf_op jit(solution)/shard_map/ppermute | solution.py:217
  678.8 17.4 %collective-permute-done.31 = bf16[128,2048]{1,0:T(8,128)(2,1)S(1)} collective-permute-done((bf16[128,2048]{1,0:T(8,128)(2,1)S(1)}, bf16[128,2048]{1,0:T(8,128)(2,1)S(1)}, u32[]{:S(2)}, u32[]{:S(2)}) %collective-permute-start.31) | collective-permute-done | bytes 524320 | tf_op jit(solution)/shard_map/ppermute | solution.py:159
  696.8 77.8 %psum.7 = f32[4352]{0:T(1024)S(1)} all-reduce(f32[4352]{0:T(1024)S(1)} %pad_maximum_fusion.18), channel_id=1, replica_groups=mesh['fsdp'=4,'sp'=8] {'fsdp','sp'}, use_global_device_ids=true, to_apply=%region_23.24 | all-reduce | flops 4352 | bytes 34816 | tf_op jit(solution)/shard_map/psum | solution.py:456
  788.2 11.2 %copy.360 = f32[64,8,8,768]{3,1,2,0:T(8,128)} copy(f32[64,8,8,768]{3,1,0,2:T(8,128)} %convert_bitcast_fusion.4) | data formatting | bytes 25165824
  828.0 15.2 %copy.359 = f32[64,8,8,768]{3,1,2,0:T(8,128)} copy(f32[64,8,8,768]{3,2,1,0:T(8,128)} %bitcast.356) | data formatting | bytes 25165824
  843.1 11.2 %copy_convert_fusion.1 = f32[8,512,768]{2,0,1:T(8,128)} fusion(bf16[8,512,768]{2,1,0:T(8,128)(2,1)} %get-tuple-element.400), kind=kLoop, calls=%fused_computation.62 | loop fusion | flops 3145728 | bytes 18874368 | tf_op jit(solution)/shard_map/reshape | solution.py:244
  854.3 15.3 %copy.358 = f32[64,8,8,768]{3,1,2,0:T(8,128)} copy(f32[64,8,8,768]{3,2,1,0:T(8,128)} %bitcast.357) | data formatting | bytes 25165824
  (455 shorter events, 436.9 us)
Async XLA Ops:
  7.2 77.0 %all-gather.11.cloned.1.call-start = ((), (), s32[]{:S(2)}) async-start(), calls=%async_computation.1 | async-start | bytes 2621440 | tf_op jit(solution)/shard_map/all_gather | solution.py:293
  10.7 167.8 %all-gather.13.cloned.1.call-start = ((), (), s32[]{:S(2)}) async-start(), calls=%async_computation.2 | async-start | bytes 1310720 | tf_op jit(solution)/shard_map/all_gather | solution.py:294
  17.0 214.2 %all-gather.15.cloned.1.call-start = ((), (), s32[]{:S(2)}) async-start(), calls=%async_computation.3 | async-start | bytes 7864320 | tf_op jit(solution)/shard_map/all_gather | solution.py:297
  43.2 238.6 %all-gather.17.cloned.1.call-start = ((), (), s32[]{:S(2)}) async-start(), calls=%async_computation.4 | async-start | bytes 3932160 | tf_op jit(solution)/shard_map/all_gather | solution.py:309
  139.7 29.7 %collective-permute-start.7 = (bf16[4,1024,256]{2,1,0:T(8,128)(2,1)S(1)}, bf16[4,1024,256]{2,1,0:T(8,128)(2,1)S(1)}, u32[]{:S(2)}, u32[]{:S(2)}) collective-permute-start(bf16[4,1024,256]{2,1,0:T(8,128)(2,1)S(1)} %bitcast_dynamic-update-slice_fusion.9), channel_id=1, source_target_pairs={{0,1},{1,0},{2,3},{3,2},{4,5},{5,4},{6,7},{7,6},{8,9},{9,8},{10,11... | collective-permute-start | bytes 6291464 | tf_op jit(solution)/shard_map/ppermute | solution.py:159
  139.9 28.7 %collective-permute-start.18 = (bf16[128,2048]{1,0:T(8,128)(2,1)S(1)}, bf16[128,2048]{1,0:T(8,128)(2,1)S(1)}, u32[]{:S(2)}, u32[]{:S(2)}) collective-permute-start(bf16[128,2048]{1,0:T(8,128)(2,1)S(1)} %copy-done.16), channel_id=1, source_target_pairs={{0,6},{1,7},{2,4},{3,5},{4,2},{5,3},{6,0},{7,1},{8,14},{9,15},{10,... | collective-permute-start | bytes 1572872 | tf_op jit(solution)/shard_map/ppermute | solution.py:159
  169.4 49.3 %collective-permute-start.19 = (bf16[4,128,2048]{2,1,0:T(8,128)(2,1)}, bf16[4,128,2048]{2,1,0:T(8,128)(2,1)}, u32[]{:S(2)}, u32[]{:S(2)}) collective-permute-start(bf16[4,128,2048]{2,1,0:T(8,128)(2,1)} %bitcast_dynamic-update-slice_fusion.5), channel_id=1, source_target_pairs={{0,1},{1,0},{2,3},{3,2},{4,5},{5,4},{6,7},{7,6},{8,9},{9,8},{10,11... | collective-permute-start | bytes 6291464 | tf_op jit(solution)/shard_map/ppermute | solution.py:159
  183.5 25.5 %collective-permute-start.9 = (bf16[1024,256]{0,1:T(8,128)(2,1)}, bf16[1024,256]{0,1:T(8,128)(2,1)S(1)}, u32[]{:S(2)}, u32[]{:S(2)}) collective-permute-start(bf16[1024,256]{0,1:T(8,128)(2,1)} %fusion.74), channel_id=1, source_target_pairs={{0,4},{1,5},{2,6},{3,7},{4,0},{5,1},{6,2},{7,3},{8,12},{9,13},{10,... | collective-permute-start | bytes 1572872 | tf_op jit(solution)/shard_map/ppermute | solution.py:159
  185.2 25.8 %collective-permute-start.8 = (bf16[1024,256]{0,1:T(8,128)(2,1)}, bf16[1024,256]{0,1:T(8,128)(2,1)}, u32[]{:S(2)}, u32[]{:S(2)}) collective-permute-start(bf16[1024,256]{0,1:T(8,128)(2,1)} %fusion.74), channel_id=1, source_target_pairs={{0,2},{1,3},{2,0},{3,1},{4,6},{5,7},{6,4},{7,5},{8,10},{9,11},{10,... | collective-permute-start | bytes 1572872 | tf_op jit(solution)/shard_map/ppermute | solution.py:159
  319.2 27.0 %collective-permute-start.42 = (bf16[512,768]{1,0:T(8,128)(2,1)}, bf16[512,768]{1,0:T(8,128)(2,1)}, u32[]{:S(2)}, u32[]{:S(2)}) collective-permute-start(bf16[512,768]{1,0:T(8,128)(2,1)} %dynamic-slice_bitcast_fusion.5), channel_id=1, source_target_pairs={{0,8},{24,16},{1,9},{25,17},{2,10},{26,18},{3,11},{27,19},{4,12},{... | collective-permute-start | bytes 2359304 | tf_op jit(solution)/shard_map/ppermute | solution.py:214
  348.6 25.9 %collective-permute-start.45 = (bf16[512,768]{1,0:T(8,128)(2,1)}, bf16[512,768]{1,0:T(8,128)(2,1)}, u32[]{:S(2)}, u32[]{:S(2)}) collective-permute-start(bf16[512,768]{1,0:T(8,128)(2,1)} %fusion.59), channel_id=1, source_target_pairs={{16,8},{24,16},{17,9},{25,17},{18,10},{26,18},{19,11},{27,19},{20,... | collective-permute-start | bytes 2359304 | tf_op jit(solution)/shard_map/ppermute | solution.py:220
  370.1 35.0 %collective-permute-start.27 = (bf16[4,128,2048]{2,1,0:T(8,128)(2,1)}, bf16[4,128,2048]{2,1,0:T(8,128)(2,1)}, u32[]{:S(2)}, u32[]{:S(2)}) collective-permute-start(bf16[4,128,2048]{2,1,0:T(8,128)(2,1)} %bitcast_dynamic-update-slice_fusion.1), channel_id=1, source_target_pairs={{0,1},{1,0},{2,3},{3,2},{4,5},{5,4},{6,7},{7,6},{8,9},{9,8},{10,11... | collective-permute-start | bytes 6291464 | tf_op jit(solution)/shard_map/ppermute | solution.py:159
  374.4 405.1 %all-gather.23.cloned.1.call-start = ((), (), s32[]{:S(2)}) async-start(), calls=%async_computation.7 | async-start | bytes 7077888 | tf_op jit(solution)/shard_map/all_gather | solution.py:238
  405.1 394.3 %all-gather.19.cloned.1.call-start = ((), (), s32[]{:S(2)}) async-start(), calls=%async_computation.5 | async-start | bytes 7077888 | tf_op jit(solution)/shard_map/all_gather | solution.py:238
  521.6 289.2 %all-gather.21.cloned.1.call-start = ((), (), s32[]{:S(2)}) async-start(), calls=%async_computation.6 | async-start | bytes 14155776 | tf_op jit(solution)/shard_map/all_gather | solution.py:238
  531.6 33.6 %collective-permute-start.37 = (bf16[512,1536]{1,0:T(8,128)(2,1)S(1)}, bf16[512,1536]{1,0:T(8,128)(2,1)S(1)}, u32[]{:S(2)}, u32[]{:S(2)}) collective-permute-start(bf16[512,1536]{1,0:T(8,128)(2,1)S(1)} %dynamic-slice_bitcast_fusion.4), channel_id=1, source_target_pairs={{0,8},{24,16},{1,9},{25,17},{2,10},{26,18},{3,11},{27,19},{4,12},{... | collective-permute-start | bytes 4718600 | tf_op jit(solution)/shard_map/ppermute | solution.py:214
  566.4 34.1 %collective-permute-start.38 = (bf16[512,1536]{1,0:T(8,128)(2,1)S(1)}, bf16[512,1536]{1,0:T(8,128)(2,1)S(1)}, u32[]{:S(2)}, u32[]{:S(2)}) collective-permute-start(bf16[512,1536]{1,0:T(8,128)(2,1)S(1)} %fusion.53), channel_id=1, source_target_pairs={{0,8},{8,16},{1,9},{9,17},{2,10},{10,18},{3,11},{11,19},{4,12},{12... | collective-permute-start | bytes 4718600 | tf_op jit(solution)/shard_map/ppermute | solution.py:217
  601.5 32.8 %collective-permute-start.39 = (bf16[512,1536]{1,0:T(8,128)(2,1)S(1)}, bf16[512,1536]{1,0:T(8,128)(2,1)S(1)}, u32[]{:S(2)}, u32[]{:S(2)}) collective-permute-start(bf16[512,1536]{1,0:T(8,128)(2,1)S(1)} %get-tuple-element.403), channel_id=1, source_target_pairs={{0,8},{8,16},{16,24},{1,9},{9,17},{17,25},{2,10},{10,18},{18,26},{... | collective-permute-start | bytes 4718600 | tf_op jit(solution)/shard_map/ppermute | solution.py:217
  606.2 32.5 %collective-permute-start.41 = (bf16[512,1536]{1,0:T(8,128)(2,1)S(1)}, bf16[512,1536]{1,0:T(8,128)(2,1)S(1)}, u32[]{:S(2)}, u32[]{:S(2)}) collective-permute-start(bf16[512,1536]{1,0:T(8,128)(2,1)S(1)} %get-tuple-element.404), channel_id=1, source_target_pairs={{8,0},{16,8},{24,16},{9,1},{17,9},{25,17},{10,2},{18,10},{26,18},{... | collective-permute-start | bytes 4718600 | tf_op jit(solution)/shard_map/ppermute | solution.py:220
  660.0 36.2 %collective-permute-start.31 = (bf16[128,2048]{1,0:T(8,128)(2,1)S(1)}, bf16[128,2048]{1,0:T(8,128)(2,1)S(1)}, u32[]{:S(2)}, u32[]{:S(2)}) collective-permute-start(bf16[128,2048]{1,0:T(8,128)(2,1)S(1)} %get-tuple-element.427), channel_id=1, source_target_pairs={{0,6},{1,7},{2,4},{3,5},{4,2},{5,3},{6,0},{7,1},{8,14},{9,15},{10,... | collective-permute-start | bytes 1572872 | tf_op jit(solution)/shard_map/ppermute | solution.py:159
  660.7 35.5 %collective-permute-start.30 = (bf16[128,2048]{1,0:T(8,128)(2,1)S(1)}, bf16[128,2048]{1,0:T(8,128)(2,1)S(1)}, u32[]{:S(2)}, u32[]{:S(2)}) collective-permute-start(bf16[128,2048]{1,0:T(8,128)(2,1)S(1)} %get-tuple-element.428), channel_id=1, source_target_pairs={{0,4},{1,5},{2,6},{3,7},{4,0},{5,1},{6,2},{7,3},{8,12},{9,13},{10,... | collective-permute-start | bytes 1572872 | tf_op jit(solution)/shard_map/ppermute | solution.py:159
  667.1 108.7 %collective-permute-start.13 = (bf16[128,2048]{1,0:T(8,128)(2,1)}, bf16[128,2048]{1,0:T(8,128)(2,1)}, u32[]{:S(2)}, u32[]{:S(2)}) collective-permute-start(bf16[128,2048]{1,0:T(8,128)(2,1)} %get-tuple-element.432), channel_id=1, source_target_pairs={{0,2},{1,3},{2,0},{3,1},{4,6},{5,7},{6,4},{7,5},{8,10},{9,11},{10,... | collective-permute-start | bytes 1572872 | tf_op jit(solution)/shard_map/ppermute | solution.py:159
  667.1 108.6 %collective-permute-start.15 = (bf16[128,2048]{1,0:T(8,128)(2,1)}, bf16[128,2048]{1,0:T(8,128)(2,1)}, u32[]{:S(2)}, u32[]{:S(2)}) collective-permute-start(bf16[128,2048]{1,0:T(8,128)(2,1)} %get-tuple-element.433), channel_id=1, source_target_pairs={{0,6},{1,7},{2,4},{3,5},{4,2},{5,3},{6,0},{7,1},{8,14},{9,15},{10,... | collective-permute-start | bytes 1572872 | tf_op jit(solution)/shard_map/ppermute | solution.py:159
  677.3 98.4 %collective-permute-start.14 = (bf16[128,2048]{1,0:T(8,128)(2,1)}, bf16[128,2048]{1,0:T(8,128)(2,1)}, u32[]{:S(2)}, u32[]{:S(2)}) collective-permute-start(bf16[128,2048]{1,0:T(8,128)(2,1)} %get-tuple-element.434), channel_id=1, source_target_pairs={{0,4},{1,5},{2,6},{3,7},{4,0},{5,1},{6,2},{7,3},{8,12},{9,13},{10,... | collective-permute-start | bytes 1572872 | tf_op jit(solution)/shard_map/ppermute | solution.py:159
  (98 other events, 1198.1 us)
Sparse Core Ops, SparseCore 0:
  10.8 48.5 all-gather.10
  61.5 26.7 all-gather.12
  90.5 114.6 all-gather.14
  218.8 62.9 all-gather.16
  405.2 44.1 all-gather.22
  521.7 43.7 all-gather.18
  640.5 107.7 all-gather.20

commit v2 on v1

v2 whole, which is shorter than its diff:
```python
import functools

import jax
import jax.numpy as jnp
from jax import lax
from jax.experimental import pallas as pl
from jax.experimental.layout import Layout, with_layout_constraint
from jax.experimental.pallas import tpu as pltpu
from jax.sharding import PartitionSpec as P


QUERY_HEADS = 16
KEY_VALUE_HEADS = 8
HEAD_DIMENSION = 128
LINE = 4
PLANE = 8
FSDP = "fsdp"
SP = "sp"

epsilon = 1e-06
rope_base = 1000000.0
single_precision = jnp.float32
reduced_precision = jnp.bfloat16


def contract_last(left_side, right_side):
    return lax.dot_general(
        left_side, right_side, (((1,), (1,)), ((), ())), preferred_element_type=single_precision
    )


def contract_first(left_side, right_side):
    return lax.dot_general(
        left_side, right_side, (((0,), (0,)), ((), ())), preferred_element_type=single_precision
    )


def matmul(left_side, right_side):
    return jnp.dot(left_side, right_side, preferred_element_type=single_precision)


def tie(*values):
    return lax.optimization_barrier(values)


def rope_tables(places):
    half_dim = HEAD_DIMENSION // 2
    frequency = jnp.power(
        rope_base, -(jnp.arange(half_dim, dtype=single_precision) * (2.0 / HEAD_DIMENSION))
    )
    angles = places[:, None] * frequency[None, :]
    cosine, sine = jnp.cos(angles), jnp.sin(angles)
    return jnp.concatenate([cosine, cosine], axis=1), jnp.concatenate([-sine, sine], axis=1)


def rotate(values, cosine, signed_sine):
    return values * cosine + pltpu.roll(values, HEAD_DIMENSION // 2, 1) * signed_sine


def unrotate(values, cosine, signed_sine):
    return values * cosine - pltpu.roll(values, HEAD_DIMENSION // 2, 1) * signed_sine


def inverse_norm(values):
    return lax.rsqrt(jnp.mean(values * values, axis=-1, keepdims=True) + epsilon)


def norm_backward(grad_hat, normed, inverse):
    return inverse * (grad_hat - normed * jnp.mean(grad_hat * normed, axis=-1, keepdims=True))


def token_places(seg_row):
    doc_starts = jnp.sum((seg_row[None, :] < seg_row[:, None]).astype(jnp.int32), axis=1)
    positions = jnp.arange(seg_row.shape[0], dtype=jnp.int32)
    return (positions - doc_starts).astype(single_precision)


def flip_permute(piece, axis, flip):
    size = lax.axis_size(axis)
    return lax.ppermute(piece, axis, [(i, i ^ flip) for i in range(size)])


def line_order(blocks):
    if len(blocks) != LINE:
        return blocks
    index = lax.axis_index(FSDP)
    odd, high = index % 2 == 1, index // 2 == 1
    near = [jnp.where(odd, blocks[i ^ 1], blocks[i]) for i in range(LINE)]
    return [jnp.where(high, near[i ^ 2], near[i]) for i in range(LINE)]


def line_columns(values):
    lines = lax.axis_size(FSDP)
    if lines != LINE:
        return values
    return jnp.concatenate(line_order(jnp.split(values, lines, axis=1)), axis=1)


def line_gather(piece):
    if lax.axis_size(FSDP) != LINE:
        return list(lax.all_gather(piece, FSDP, axis=0))
    index = lax.axis_index(FSDP)
    second = flip_permute(piece, FSDP, 2)
    first = flip_permute(piece, FSDP, 1)
    inner = lax.ppermute(piece, FSDP, [(1, 2), (2, 1)])
    outer = lax.ppermute(second, FSDP, [(2, 3), (1, 0)])
    third = jnp.where((index == 1) | (index == 2), inner, outer)
    return [piece, first, second, third]


def line_reduce(parts):
    if lax.axis_size(FSDP) != LINE:
        return lax.psum_scatter(jnp.stack(parts), FSDP, scatter_dimension=0, tiled=False)

    def wide(part):
        return part.astype(single_precision)

    kind = parts[0].dtype
    outer = lax.ppermute(parts[3], FSDP, [(3, 2), (0, 1)])
    inner = lax.ppermute(parts[3], FSDP, [(1, 2), (2, 1)])
    first = flip_permute(parts[1], FSDP, 1)
    second = flip_permute((wide(parts[2]) + wide(outer)).astype(kind), FSDP, 2)
    return (wide(parts[0]) + wide(first) + wide(inner) + wide(second)).astype(kind)


def row_parts(left, right):
    parts = []
    for block in jnp.split(left, lax.axis_size(FSDP), axis=1):
        parts.append(contract_first(block, right).astype(reduced_precision))
    return parts


def unsummed(parts):
    return parts[:2] + parts[3:]


def plane_rows(piece):
    return lax.all_gather(piece, SP, axis=0, tiled=True)


def joining_kernel(count, order, *refs):
    pieces, gain, outs = refs[:count], refs[count], refs[count + 1 :]
    whole = jnp.concatenate([piece[0] for piece in pieces], axis=1)
    outs[0][...] = whole
    if len(outs) > 1:
        wide = whole.astype(single_precision)
        outs[1][...] = (wide * inverse_norm(wide) * gain[...]).astype(reduced_precision)


def plane_columns(piece, gain, normed):
    plane, lines = lax.axis_size(SP), lax.axis_size(FSDP)
    pieces = lax.all_gather(piece, SP, axis=0)
    rows, width = piece.shape
    order = jnp.arange(plane, dtype=jnp.int32)
    if lines == LINE:
        order = order ^ (lax.axis_index(FSDP) * (plane // lines))
    tile = 128

    def from_piece(at):
        return pl.BlockSpec((1, tile, width), lambda row, order: (order[at], row, 0))

    whole = pl.BlockSpec((tile, plane * width), lambda row, order: (row, 0))
    count = 2 if normed else 1
    return pl.pallas_call(
        functools.partial(joining_kernel, plane),
        out_shape=[jax.ShapeDtypeStruct((rows, plane * width), piece.dtype)] * count,
        grid_spec=pltpu.PrefetchScalarGridSpec(
            num_scalar_prefetch=1,
            grid=(rows // tile,),
            in_specs=[from_piece(at) for at in range(plane)]
            + [pl.BlockSpec((1, plane * width), lambda row, order: (0, 0))],
            out_specs=[whole] * count,
        ),
    )(order, *[pieces] * plane, gain)


def plane_reduce(parts):
    if lax.axis_size(SP) != PLANE:
        return lax.psum_scatter(parts, SP, scatter_dimension=0, tiled=False).astype(
            single_precision
        )
    index = lax.axis_index(SP)
    chip, core = index // 2, index % 2
    split = parts.reshape((4, 2) + parts.shape[1:])
    given = lax.dynamic_index_in_dim(split, 1 - core, 1, keepdims=False)
    kept = lax.dynamic_index_in_dim(split, core, 1, keepdims=False)
    other = flip_permute(given, SP, 1)
    joined = (kept.astype(single_precision) + other.astype(single_precision)).astype(
        reduced_precision
    )
    total = lax.dynamic_index_in_dim(joined, chip, 0, keepdims=False).astype(single_precision)
    for turn in (1, 2, 3):
        sent = lax.dynamic_index_in_dim(joined, chip ^ turn, 0, keepdims=False)
        found = flip_permute(sent, SP, 2 * turn)
        total = total + found.astype(single_precision)
    return total


def columns_of(weight, first, width):
    return lax.dynamic_slice_in_dim(weight, first, width, 1)


def widening_kernel(widths, piece, *outs):
    offset = 0
    for width, out in zip(widths, outs):
        out[...] = piece[0, :, offset : offset + width].astype(out.dtype)
        offset = offset + width


def spread(reduced, widths):
    size = lax.axis_size(SP)
    rows, total = reduced.shape
    reduced = with_layout_constraint(reduced, Layout(major_to_minor=(0, 1)))
    everything = lax.all_gather(reduced, SP, axis=0)
    tile = 256
    if all(width % 128 == 0 for width in widths) and rows % tile == 0:
        return pl.pallas_call(
            functools.partial(widening_kernel, widths),
            grid=(rows // tile, size),
            out_shape=[
                jax.ShapeDtypeStruct((rows, size * width), single_precision)
                for width in widths
            ],
            in_specs=[pl.BlockSpec((1, tile, total), lambda row, at: (at, row, 0))],
            out_specs=[pl.BlockSpec((tile, width), lambda row, at: (row, at)) for width in widths],
        )(everything)
    results = []
    offset = 0
    for width in widths:
        piece = everything[:, :, offset : offset + width].astype(single_precision)
        results.append(jnp.transpose(piece, (1, 0, 2)).reshape(rows, size * width))
        offset = offset + width
    return results


def projecting_kernel(heads, count, x, gain, query_gain, key_gain, cosine, sine, *refs):
    blocks, (normed_out, raw_out, turned_out) = refs[:count], refs[count:]
    wide = x[...].astype(single_precision)
    normed = (wide * inverse_norm(wide) * gain[...]).astype(reduced_precision)
    normed_out[...] = normed
    depth = blocks[0].shape[0]
    total = matmul(normed[:, :depth], blocks[0][...])
    for at in range(1, count):
        total = total + matmul(normed[:, at * depth : (at + 1) * depth], blocks[at][...])
    raw_out[...] = total[:, : (heads + 1) * HEAD_DIMENSION]
    for head in range(heads + 2):
        window = slice(head * HEAD_DIMENSION, (head + 1) * HEAD_DIMENSION)
        values = total[:, window]
        if head <= heads:
            head_gain = query_gain if head < heads else key_gain
            values = rotate(
                values * inverse_norm(values) * head_gain[...], cosine[...], sine[...]
            )
        turned_out[:, window] = values.astype(reduced_precision)


def project(x, gain, blocks, query_gain, key_gain, cosine, sine, heads):
    length, width = x.shape
    count = len(blocks)
    columns = blocks[0].shape[1]
    depth = width // count
    tile = 256

    def rows(size):
        return pl.BlockSpec((tile, size), lambda row: (row, 0))

    def fixed(*shape):
        return pl.BlockSpec(shape, lambda row: (0, 0))

    return pl.pallas_call(
        functools.partial(projecting_kernel, heads, count),
        grid=(length // tile,),
        out_shape=[
            jax.ShapeDtypeStruct((length, width), reduced_precision),
            jax.ShapeDtypeStruct((length, columns - HEAD_DIMENSION), single_precision),
            jax.ShapeDtypeStruct((length, columns), reduced_precision),
        ],
        in_specs=[
            rows(width),
            fixed(1, width),
            fixed(1, HEAD_DIMENSION),
            fixed(1, HEAD_DIMENSION),
            rows(HEAD_DIMENSION),
            rows(HEAD_DIMENSION),
        ]
        + [fixed(depth, columns)] * count,
        out_specs=[rows(width), rows(columns - HEAD_DIMENSION), rows(columns)],
    )(x, gain, query_gain, key_gain, cosine, sine, *blocks)


SCORE_SCALE = HEAD_DIMENSION ** (-0.5)


def allowed_pairs(first, tile, reach, seg_col, seg_row):
    query_place = first + lax.broadcasted_iota(jnp.int32, (tile, reach), 0)
    key_place = lax.broadcasted_iota(jnp.int32, (tile, reach), 1)
    return (key_place <= query_place) & (seg_col[...] == seg_row[:, :reach])


def attending_kernel(blocks, query, key, value, seg_col, seg_row, out, log_total):
    tile = query.shape[0]
    for block in range(blocks):

        @pl.when(pl.program_id(1) == block)
        def _():
            reach = (block + 1) * tile
            scores = contract_last(query[...], key[:reach, :]) * SCORE_SCALE
            allowed = allowed_pairs(block * tile, tile, reach, seg_col, seg_row)
            scores = jnp.where(allowed, scores, -1e30)
            top = jnp.max(scores, axis=1, keepdims=True)
            powers = jnp.exp(scores - top)
            total = jnp.sum(powers, axis=1, keepdims=True)
            probs = (powers * (1.0 / total)).astype(reduced_precision)
            out[...] = matmul(probs, value[:reach, :]).astype(reduced_precision)
            log_total[0] = top + jnp.log(total)


def attend(turned, seg_row, heads):
    length = turned.shape[0]
    tile = 256
    blocks = length // tile
    return pl.pallas_call(
        functools.partial(attending_kernel, blocks),
        grid=(heads, blocks),
        out_shape=[
            jax.ShapeDtypeStruct((length, heads * HEAD_DIMENSION), reduced_precision),
            jax.ShapeDtypeStruct((heads, length, 1), single_precision),
        ],
        in_specs=[
            pl.BlockSpec((tile, HEAD_DIMENSION), lambda head, row: (row, head)),
            pl.BlockSpec((length, HEAD_DIMENSION), lambda head, row: (0, heads)),
            pl.BlockSpec((length, HEAD_DIMENSION), lambda head, row: (0, heads + 1)),
            pl.BlockSpec((tile, 1), lambda head, row: (row, 0)),
            pl.BlockSpec((1, length), lambda head, row: (0, 0)),
        ],
        out_specs=[
            pl.BlockSpec((tile, HEAD_DIMENSION), lambda head, row: (row, head)),
            pl.BlockSpec((1, tile, 1), lambda head, row: (head, row, 0)),
        ],
    )(turned, turned, turned, seg_row[:, None], seg_row[None, :])


def attending_back_kernel(
    heads,
    blocks,
    finish,
    query,
    key,
    value,
    out,
    out_grad,
    log_total,
    seg_col,
    seg_row,
    query_raw,
    key_raw,
    cosine,
    sine,
    query_gain,
    key_gain,
    query_lin,
    key_out,
    value_out,
    query_part,
    key_part,
    key_sum,
    value_sum,
):
    tile = query.shape[0]
    head, row = pl.program_id(0), pl.program_id(1)

    @pl.when((head == 0) & (row == 0))
    def _():
        key_sum[...] = jnp.zeros_like(key_sum)
        value_sum[...] = jnp.zeros_like(value_sum)
        query_part[...] = jnp.zeros_like(query_part)
        key_part[...] = jnp.zeros_like(key_part)

    def backward(grads, raw, cos_part, sin_part, gain):
        turn = unrotate(grads, cos_part, sin_part)
        inverse = inverse_norm(raw)
        hat = raw * inverse
        part = jnp.sum(turn * hat, axis=0, keepdims=True)
        return norm_backward(turn * gain[...], hat, inverse).astype(reduced_precision), part

    for block in range(blocks):

        @pl.when(row == block)
        def _():
            reach = (block + 1) * tile
            window = slice(block * tile, reach)
            queries, grads, keys = query[...], out_grad[...], key[:reach, :]
            scores = contract_last(queries, keys) * SCORE_SCALE
            allowed = allowed_pairs(block * tile, tile, reach, seg_col, seg_row)
            probs = jnp.where(allowed, jnp.exp(scores - log_total[0]), 0.0)
            value_sum[:reach, :] += contract_first(probs.astype(reduced_precision), grads)
            prob_grads = contract_last(grads, value[:reach, :])
            delta = jnp.sum(
                grads.astype(single_precision) * out[...].astype(single_precision),
                axis=1,
                keepdims=True,
            )
            score_grads = (probs * (prob_grads - delta) * SCORE_SCALE).astype(reduced_precision)
            back = matmul(score_grads, keys)
            key_sum[:reach, :] += contract_first(score_grads, queries)
            lin, part = backward(
                back, query_raw[...], cosine[window, :], sine[window, :], query_gain
            )
            query_lin[...] = lin
            query_part[...] += part

    @pl.when((head == heads - 1) & (row == blocks - 1))
    def _():
        if finish:
            lin, part = backward(key_sum[...], key_raw[...], cosine[...], sine[...], key_gain)
            key_out[...] = lin
            key_part[...] = part
        else:
            key_out[...] = key_sum[...]
        value_out[...] = value_sum[...].astype(value_out.dtype)


def attend_back(
    turned, attended, out_grads, log_totals, seg_row, raw, cosine, sine, gains, heads, finish
):
    length = turned.shape[0]
    tile = 256
    blocks = length // tile
    kind = reduced_precision if finish else single_precision
    one_head = pl.BlockSpec((tile, HEAD_DIMENSION), lambda head, row: (row, head))

    def whole(column):
        return pl.BlockSpec((length, HEAD_DIMENSION), lambda head, row: (0, column))

    vector = pl.BlockSpec((1, HEAD_DIMENSION), lambda head, row: (0, 0))
    return pl.pallas_call(
        functools.partial(attending_back_kernel, heads, blocks, finish),
        grid=(heads, blocks),
        out_shape=[
            jax.ShapeDtypeStruct((length, heads * HEAD_DIMENSION), reduced_precision),
            jax.ShapeDtypeStruct((length, HEAD_DIMENSION), kind),
            jax.ShapeDtypeStruct((length, HEAD_DIMENSION), kind),
            jax.ShapeDtypeStruct((1, HEAD_DIMENSION), single_precision),
            jax.ShapeDtypeStruct((1, HEAD_DIMENSION), single_precision),
        ],
        in_specs=[
            one_head,
            whole(heads),
            whole(heads + 1),
            one_head,
            one_head,
            pl.BlockSpec((1, tile, 1), lambda head, row: (head, row, 0)),
            pl.BlockSpec((tile, 1), lambda head, row: (row, 0)),
            pl.BlockSpec((1, length), lambda head, row: (0, 0)),
            one_head,
            whole(heads),
            whole(0),
            whole(0),
            vector,
            vector,
        ],
        out_specs=[one_head, whole(0), whole(0), vector, vector],
        scratch_shapes=[pltpu.VMEM((length, HEAD_DIMENSION), single_precision)] * 2,
    )(
        turned,
        turned,
        turned,
        attended,
        out_grads,
        log_totals,
        seg_row[:, None],
        seg_row[None, :],
        raw,
        raw,
        cosine,
        sine,
        *gains,
    )


def sum_plane(values):
    turn = 1
    while turn < lax.axis_size(SP):
        values = values + flip_permute(values, SP, turn)
        turn = 2 * turn
    return values


def on_device(
    tokens,
    segments,
    prenorm,
    query_proj,
    key_projection,
    value_projection,
    query_norm,
    key_norm_gain,
    output_proj,
    postnorm,
    gate_proj,
    up_proj,
    down_proj,
    out_grad,
):
    token_rows, model_width = tokens.shape
    plane = lax.axis_size(SP)
    lines = lax.axis_size(FSDP)
    spot = lax.axis_index(SP)
    line = lax.axis_index(FSDP)
    seg_row = segments[0]
    heads = QUERY_HEADS // plane
    query_width = heads * HEAD_DIMENSION
    share = max(1, plane // KEY_VALUE_HEADS)
    owned = HEAD_DIMENSION // share
    model_cols = model_width // plane
    ff_cols = gate_proj.shape[1] // plane
    row_block = model_width // lines
    own_place = spot
    if lines == LINE:
        own_place = spot ^ (line * (plane // lines))

    kv_first = (spot // share) * HEAD_DIMENSION
    qkv_slice = jnp.concatenate(
        [
            columns_of(query_proj, spot * query_width, query_width),
            columns_of(key_projection, kv_first, HEAD_DIMENSION),
            columns_of(value_projection, kv_first, HEAD_DIMENSION),
        ],
        axis=1,
    )
    qkv_width = qkv_slice.shape[1]
    both_gains = jnp.pad(
        jnp.stack([prenorm, postnorm]), ((0, 14), (0, qkv_width - row_block))
    )
    qkv_blocks = line_gather(jnp.concatenate([qkv_slice, both_gains], axis=0))
    out_blocks = line_gather(columns_of(output_proj, spot * model_cols, model_cols))
    own_tokens = line_columns(tokens)
    own_grads = line_columns(out_grad)
    everyone = plane_rows(own_tokens)
    grads_all = plane_rows(own_grads)
    gate_up_slice = jnp.concatenate(
        [
            columns_of(gate_proj, spot * ff_cols, ff_cols),
            columns_of(up_proj, spot * ff_cols, ff_cols),
        ],
        axis=1,
    )
    wide_blocks = line_gather(gate_up_slice)
    down_blocks = line_gather(columns_of(down_proj, spot * ff_cols, ff_cols))

    def gain_row(at):
        return jnp.concatenate(
            [block[row_block + at : row_block + at + 1, :row_block] for block in qkv_blocks], axis=1
        ).astype(single_precision)

    prenorm_full, postnorm_full = gain_row(0), gain_row(1)
    cosine, sine = rope_tables(token_places(seg_row))
    query_gain = query_norm.astype(single_precision)[None, :]
    key_gain = key_norm_gain.astype(single_precision)[None, :]
    first_norm, raw, turned = project(
        everyone, prenorm_full, qkv_blocks, query_gain, key_gain, cosine, sine, heads
    )
    attended, log_totals = attend(turned, seg_row, heads)
    (attn_all,) = plane_columns(attended, prenorm_full, False)
    out_cols = jnp.concatenate(out_blocks, axis=0)
    middle_cols = matmul(attn_all, out_cols)
    middle_cols = middle_cols + columns_of(
        everyone, own_place * model_cols, model_cols
    ).astype(single_precision)
    middle_all, second_norm = plane_columns(
        middle_cols.astype(reduced_precision), postnorm_full, True
    )
    middle_own = lax.dynamic_slice_in_dim(middle_all, spot * token_rows, token_rows, 0).astype(
        single_precision
    )
    inv_two_own = inverse_norm(middle_own)
    hat_two_own = middle_own * inv_two_own

    gate_up = jnp.concatenate(wide_blocks, axis=0)
    gate_up_val = matmul(second_norm, gate_up)
    gate_val = gate_up_val[:, :ff_cols]
    up_val = gate_up_val[:, ff_cols:]
    sigmoid_val = jax.nn.sigmoid(gate_val)
    silu_val = gate_val * sigmoid_val
    hidden = (silu_val * up_val).astype(reduced_precision)
    down_parts = row_parts(grads_all, hidden)
    down_cols = jnp.concatenate(down_blocks, axis=0)
    down_cols, *_ = tie(down_cols, *unsummed(down_parts))
    down_sum = line_reduce(down_parts)
    hidden_grad = matmul(grads_all, down_cols)
    gate_grad = (
        hidden_grad * up_val * (sigmoid_val * (1.0 + gate_val * (1.0 - sigmoid_val)))
    ).astype(reduced_precision)
    up_grads = (hidden_grad * silu_val).astype(reduced_precision)
    both_grads = jnp.concatenate([gate_grad, up_grads], axis=1)
    out_pieces, _ = tie(jnp.concatenate(line_order(out_blocks), axis=0), second_norm)
    out_rows = lax.all_to_all(
        out_pieces.reshape(plane, query_width, model_cols),
        SP,
        split_axis=0,
        concat_axis=0,
        tiled=True,
    )
    both_grads, out_rows = tie(both_grads, out_rows)
    norm_two_part = contract_last(both_grads, gate_up).astype(reduced_precision)
    norm_two_grad = plane_reduce(norm_two_part.reshape(plane, token_rows, model_width))
    gate_parts = row_parts(second_norm, both_grads[:, :ff_cols])
    up_parts = row_parts(second_norm, both_grads[:, ff_cols:])
    norm_two_grad, *_ = tie(norm_two_grad, *unsummed(gate_parts), *unsummed(up_parts))
    gate_sum = line_reduce(gate_parts)
    up_sum = line_reduce(up_parts)

    postnorm_part = jnp.sum(norm_two_grad * hat_two_own, axis=0)
    middle_grad = own_grads.astype(single_precision) + norm_backward(
        norm_two_grad * postnorm_full, hat_two_own, inv_two_own
    )
    half = middle_grad.astype(reduced_precision)
    half_all = plane_rows(half)
    late_hidden, _ = tie(hidden, half)
    block_part = contract_last(late_hidden, down_cols).astype(reduced_precision)
    block_out = line_columns(
        (
            middle_own + plane_reduce(block_part.reshape(plane, token_rows, model_width))
        ).astype(reduced_precision)
    )
    out_rows = line_columns(
        jnp.transpose(out_rows.reshape(plane, query_width, model_cols), (1, 0, 2)).reshape(
            query_width, model_width
        )
    )
    attn_grad = contract_last(half_all, out_rows).astype(reduced_precision)
    query_lin, key_lin, value_lin, query_part, key_part = attend_back(
        turned,
        attended,
        attn_grad,
        log_totals,
        seg_row,
        raw,
        cosine,
        sine,
        (query_gain, key_gain),
        heads,
        share == 1,
    )
    qkv = jnp.concatenate([block[:row_block] for block in qkv_blocks], axis=0)
    if share > 1:
        groups = [
            [first + offset for offset in range(share)] for first in range(0, plane, share)
        ]
        both = jnp.concatenate([key_lin, value_lin], axis=1)
        gathered = [both]
        for turn in range(1, share):
            pairs = [
                (group[i], group[(i + turn) % share]) for group in groups for i in range(share)
            ]
            gathered.append(lax.ppermute(both, SP, pairs))
        both = sum(gathered[1:], gathered[0])
        key_sum, value_sum = both[:, :HEAD_DIMENSION], both[:, HEAD_DIMENSION:]
        key_turn = key_sum * cosine - jnp.roll(key_sum, HEAD_DIMENSION // 2, axis=1) * sine
        key_raw = raw[:, query_width:]
        key_inv = inverse_norm(key_raw)
        key_hat = key_raw * key_inv
        key_part = jnp.sum(key_turn * key_hat, axis=0, keepdims=True) / share
        own_first = (spot % share) * owned
        key_lin = columns_of(
            norm_backward(key_turn * key_gain, key_hat, key_inv).astype(reduced_precision),
            own_first,
            owned,
        )
        value_lin = columns_of(value_sum.astype(reduced_precision), own_first, owned)
        qkv = jnp.concatenate(
            [
                qkv[:, :query_width],
                columns_of(qkv, query_width + own_first, owned),
                columns_of(qkv, query_width + HEAD_DIMENSION + own_first, owned),
            ],
            axis=1,
        )
    lin = jnp.concatenate([query_lin, key_lin, value_lin], axis=1)
    qkv_sum = line_reduce(row_parts(first_norm, lin))
    norm_one_part = contract_last(lin, qkv).astype(reduced_precision)
    norm_one_grad = plane_reduce(norm_one_part.reshape(plane, token_rows, model_width))
    out_parts = row_parts(attn_all, columns_of(half_all, own_place * model_cols, model_cols))
    out_sum = line_reduce(out_parts)
    own_tok = own_tokens.astype(single_precision)
    inv_own = inverse_norm(own_tok)
    hat_own = own_tok * inv_own
    prenorm_part = jnp.sum(norm_one_grad * hat_own, axis=0)
    input_grad = (
        middle_grad + norm_backward(norm_one_grad * prenorm_full, hat_own, inv_own)
    ).astype(reduced_precision)
    input_grad = line_columns(input_grad)
    small = sum_plane(
        jnp.concatenate([prenorm_part, postnorm_part, query_part[0], key_part[0]])
    )
    heads_part = small[2 * model_width :]
    small = line_reduce(
        [
            jnp.concatenate(
                [
                    small[at * row_block : (at + 1) * row_block],
                    small[model_width + at * row_block : model_width + (at + 1) * row_block],
                    heads_part,
                ]
            )
            for at in range(lines)
        ],
    )
    grad_prenorm = small[:row_block]
    grad_postnorm = small[row_block : 2 * row_block]
    grad_querynorm = small[2 * row_block : 2 * row_block + HEAD_DIMENSION]
    grad_keynorm = small[2 * row_block + HEAD_DIMENSION :]
    grad_down, grad_gate = spread(jnp.concatenate([down_sum, gate_sum], axis=1), [ff_cols, ff_cols])
    (grad_up,) = spread(up_sum, [ff_cols])
    grad_query, grad_key, grad_value, grad_output = spread(
        jnp.concatenate([qkv_sum, out_sum], axis=1), [query_width, owned, owned, model_cols]
    )
    return (
        block_out,
        input_grad,
        grad_prenorm,
        grad_query,
        grad_key,
        grad_value,
        grad_querynorm,
        grad_keynorm,
        grad_output,
        grad_postnorm,
        grad_gate,
        grad_up,
        grad_down,
    )


def solution(mesh):
    tokens_placed = P((FSDP, SP), None)
    rows, vector = P(FSDP, None), P(FSDP)
    return jax.shard_map(
        on_device,
        mesh=mesh,
        in_specs=(
            tokens_placed,
            rows,
            vector,
            rows,
            rows,
            rows,
            P(),
            P(),
            rows,
            vector,
            rows,
            rows,
            rows,
            tokens_placed,
        ),
        out_specs=(
            tokens_placed,
            tokens_placed,
            vector,
            rows,
            rows,
            rows,
            P(),
            P(),
            rows,
            vector,
            rows,
            rows,
            rows,
        ),
        check_vma=False,
    )
```

time: 889 us -> 855 us (0.962)
  local copies, waits for them, and re-layouts: 176 us -> 25.6 us
  waiting for transfers between devices: 328 us -> 477 us
  blocking collectives: 91.2 us -> 0 us
  Pallas kernels: 0 us -> 85.3 us
  other arithmetic: 105 us -> 47.5 us
  starting transfers between devices: 73 us -> 95.2 us
  matrix products: 84.1 us -> 97.7 us
    ppermute x47 -> x55, waiting for transfers between devices: 284 us -> 462 us  [the longest x35 366 us: flip_permute(): return lax.ppermute(piece, axis, [(i, i ^ flip) for i in range(size)])]
    pallas_call x0 -> x8, Pallas kernels: none -> 85.3 us  [the longest x3 40.4 us: spread(): pl.pallas_call(functools.partial(widening_kernel, widths), grid=(rows //...]
    psum x1 -> x0, blocking collectives: 77.8 us -> none  [on_device(): lax.psum(jnp.concatenate([prenorm_part, postnorm_part, querynorm_part, ke...]
    unnamed x126 -> x110, local copies, waits for them, and re-layouts: 60.7 us -> 10.1 us
    all_gather x7 -> x8, waiting for transfers between devices: 38.3 us -> 11 us  [the longest x2 11 us: plane_columns(): pieces = lax.all_gather(piece, SP, axis=0)]
    another operation x11 -> x1, local copies, waits for them, and re-layouts: 27.2 us -> 1.04 us  [token_places(): seg_row[:, None]]
    ppermute x47 -> x55, starting transfers between devices: 68.4 us -> 90.9 us  [the longest x35 62.3 us: flip_permute(): return lax.ppermute(piece, axis, [(i, i ^ flip) for i in range(size)])]
    dot_general x4 -> x20, matrix products: 18.7 us -> 39.2 us  [contract_first(): lax.dot_general(left_side, right_side, (((0,), (0,)), ((), ())), preferre...]
  transfers between devices with their start and end apart: 55 -> 64, of which waited for: 28 -> 34; matrix products, arithmetic and copies ran while one was open for 31% -> 15% of each run, Pallas kernels for 0% -> 5%
where the time goes in v2:
time: 855 us; the launch traced here: 844 us
  waiting for transfers between devices  477 us (56%)
  matrix products  97.7 us (11%)
  starting transfers between devices  95.2 us (11%)
  Pallas kernels  85.3 us (10%)
  other arithmetic  47.5 us (6%)
  local copies, waits for them, and re-layouts  25.6 us (3%)
  between operations  15.8 us (2%)
    ppermute x35, waiting for transfers between devices, flip_permute(): return lax.ppermute(piece, axis, [(i, i ^ flip) for i in range(size)])  366 us
    ppermute x35, starting transfers between devices, flip_permute(): return lax.ppermute(piece, axis, [(i, i ^ flip) for i in range(size)])  62.3 us
    ppermute x4, waiting for transfers between devices, line_gather(): outer = lax.ppermute(second, FSDP, [(2, 3), (1, 0)])  49.3 us
    ppermute x6, waiting for transfers between devices, line_reduce(): outer = lax.ppermute(parts[3], FSDP, [(3, 2), (0, 1)])  46.5 us
    pallas_call x3, Pallas kernels, spread(): pl.pallas_call(functools.partial(widening_kernel, widths), grid=(rows //...  40.4 us
    dot_general x20, matrix products, contract_first(): lax.dot_general(left_side, right_side, (((0,), (0,)), ((), ())), preferre...  39.2 us
    dot_general x4, matrix products, contract_last(): lax.dot_general(left_side, right_side, (((1,), (1,)), ((), ())), preferre...  30.5 us
    dot_general x3, matrix products, matmul(): jnp.dot(left_side, right_side, preferred_element_type=single_precision)  28 us
  transfers between devices with their start and end apart: 64, of which 34 were waited for; matrix products, arithmetic and copies ran while one was open for 15% of the time, Pallas kernels for 5%

profile of v2, /device:TPU:0, one launch (start us, length us, event | category | flops | bytes accessed | tf_op | source)
XLA Modules:
  0.0 844.0 jit_solution(4254136620360068377)
XLA Ops:
  23.9 30.3 %collective-permute-done.1.refs_2_ = bf16[528,512]{1,0:T(8,128)(2,1)S(1)} collective-permute-done((bf16[528,512]{1,0:T(8,128)(2,1)S(1)}, bf16[528,512]{1,0:T(8,128)(2,1)S(1)}, u32[]{:S(2)}, u32[]{:S(2)}) %collective-permute-start.1) | collective-permute-done | bytes 540704 | tf_op jit(solution)/shard_map/ppermute | solution.py:80
  58.1 11.2 %collective-permute-done.3 = bf16[528,512]{1,0:T(8,128)(2,1)S(1)} collective-permute-done((bf16[528,512]{1,0:T(8,128)(2,1)S(1)}, bf16[528,512]{1,0:T(8,128)(2,1)S(1)}, u32[]{:S(2)}, u32[]{:S(2)}) %collective-permute-start.3) | collective-permute-done | bytes 540704 | tf_op jit(solution)/shard_map/ppermute | solution.py:106
  113.5 11.0 %all-gather.20.cloned.1.call-done = bf16[8192,256]{1,0:T(8,128)(2,1)} async-done(((bf16[1024,256]{1,0:T(8,128)(2,1)}), bf16[8192,256]{1,0:T(8,128)(2,1)}) %all-gather.20.cloned.1.call-update) | async-done | bytes 4194320 | tf_op jit(solution)/shard_map/all_gather | solution.py:152
  147.6 81.5 %collective-permute-done.9 = bf16[512,1536]{1,0:T(8,128)(2,1)} collective-permute-done((bf16[512,1536]{1,0:T(8,128)(2,1)}, bf16[512,1536]{1,0:T(8,128)(2,1)}, u32[]{:S(2)}, u32[]{:S(2)}) %collective-permute-start.9) | collective-permute-done | bytes 1572896 | tf_op jit(solution)/shard_map/ppermute | solution.py:80
  230.4 15.6 %collective-permute-done.13 = bf16[512,768]{1,0:T(8,128)(2,1)} collective-permute-done((bf16[512,768]{1,0:T(8,128)(2,1)S(1)}, bf16[512,768]{1,0:T(8,128)(2,1)}, u32[]{:S(2)}, u32[]{:S(2)}) %collective-permute-start.13) | collective-permute-done | bytes 786464 | tf_op jit(solution)/shard_map/ppermute | solution.py:80
  252.4 11.1 %collective-permute-start.8 = (bf16[512,1536]{1,0:T(8,128)(2,1)}, bf16[512,1536]{1,0:T(8,128)(2,1)}, u32[]{:S(2)}, u32[]{:S(2)}) collective-permute-start(bf16[512,1536]{1,0:T(8,128)(2,1)} %pad_maximum_fusion.3), channel_id=1, source_target_pairs={{0,8},{8,0},{16,24},{24,16},{1,9},{9,1},{17,25},{25,17},{2,10},{10... | collective-permute-start | bytes 4718600 | tf_op jit(solution)/shard_map/ppermute | solution.py:80
  266.0 29.9 %collective-permute-done.15 = bf16[512,768]{1,0:T(8,128)(2,1)} collective-permute-done((bf16[512,768]{1,0:T(8,128)(2,1)}, bf16[512,768]{1,0:T(8,128)(2,1)}, u32[]{:S(2)}, u32[]{:S(2)}) %collective-permute-start.15) | collective-permute-done | bytes 786464 | tf_op jit(solution)/shard_map/ppermute | solution.py:106
  297.1 15.6 %collective-permute-done.12 = bf16[512,768]{1,0:T(8,128)(2,1)} collective-permute-done((bf16[512,768]{1,0:T(8,128)(2,1)S(1)}, bf16[512,768]{1,0:T(8,128)(2,1)}, u32[]{:S(2)}, u32[]{:S(2)}) %collective-permute-start.12) | collective-permute-done | bytes 786464 | tf_op jit(solution)/shard_map/ppermute | solution.py:80
  327.7 18.6 %collective-permute-done.8 = bf16[512,1536]{1,0:T(8,128)(2,1)} collective-permute-done((bf16[512,1536]{1,0:T(8,128)(2,1)}, bf16[512,1536]{1,0:T(8,128)(2,1)}, u32[]{:S(2)}, u32[]{:S(2)}) %collective-permute-start.8) | collective-permute-done | bytes 1572896 | tf_op jit(solution)/shard_map/ppermute | solution.py:80
  346.4 14.5 %fusion.119 = f32[1024,1536]{1,0:T(8,128)S(1)} fusion(bf16[1024,2048]{1,0:T(8,128)(2,1)} %get-tuple-element.40, bf16[512,1536]{1,0:T(8,128)(2,1)} %broadcast_select_fusion, bf16[512,1536]{1,0:T(8,128)(2,1)} %collective-permute-done.9, bf16[512,1536]{1,0:T(8,128)(2,1)} %collective-permute-done.8, bf16[512,768]{1,0:T(8,128)(2,1)S(1)} %get-tuple-element.138, ...), kind=kOutput, calls=%fused_computation.279 | convolution fusion | flops 6473908224 | bytes 16777216 | tf_op jit(solution)/shard_map/dot_general | solution.py:39
  392.3 14.1 %convolution_convert_fusion = bf16[1024,2048]{1,0:T(8,128)(2,1)S(1)} fusion(bf16[1024,1536]{1,0:T(8,128)(2,1)} %pad_maximum_fusion.2, bf16[512,1536]{1,0:T(8,128)(2,1)} %broadcast_select_fusion, bf16[512,1536]{1,0:T(8,128)(2,1)} %collective-permute-done.9, bf16[512,1536]{1,0:T(8,128)(2,1)} %collective-permute-done.8, ...), kind=kOutput, calls=%fused_computation.8 | convolution fusion | flops 6476005376 | bytes 13631488 | tf_op jit(solution)/shard_map/dot_general | solution.py:27
  459.0 14.4 %collective-permute-done.53 = bf16[512,768]{1,0:T(8,128)(2,1)S(1)} collective-permute-done((bf16[512,768]{1,0:T(8,128)(2,1)}, bf16[512,768]{1,0:T(8,128)(2,1)S(1)}, u32[]{:S(2)}, u32[]{:S(2)}) %collective-permute-start.53) | collective-permute-done | bytes 786464 | tf_op jit(solution)/shard_map/ppermute | solution.py:119
  490.3 22.1 %collective-permute-done.54 = bf16[512,768]{1,0:T(8,128)(2,1)S(1)} collective-permute-done((bf16[512,768]{1,0:T(8,128)(2,1)S(1)}, bf16[512,768]{1,0:T(8,128)(2,1)S(1)}, u32[]{:S(2)}, u32[]{:S(2)}) %collective-permute-start.54) | collective-permute-done | bytes 786464 | tf_op jit(solution)/shard_map/ppermute | solution.py:80
  523.8 12.1 %shard_map.241 = (bf16[1024,256]{1,0:T(8,128)(2,1)}, bf16[1024,128]{1,0:T(8,128)(2,1)}, bf16[1024,128]{1,0:T(8,128)(2,1)}, f32[1,128]{1,0:T(1,128)}, f32[1,128]{1,0:T(1,128)}) custom-call(bf16[1024,512]{1,0:T(8,128)(2,1)} %get-tuple-element.37.query.key.value, bf16[1024,512]{1,0:T(8,128)(2,1)} %get-tuple-element.37.query.key.value, ...), custom_call_target="tpu_custom_call" | custom-call | tf_op jit(solution)/shard_map/pallas_call | solution.py:436
  596.9 15.3 %collective-permute-done.45 = bf16[512,768]{1,0:T(8,128)(2,1)S(1)} collective-permute-done((bf16[512,768]{1,0:T(8,128)(2,1)}, bf16[512,768]{1,0:T(8,128)(2,1)S(1)}, u32[]{:S(2)}, u32[]{:S(2)}) %collective-permute-start.45) | collective-permute-done | bytes 786464 | tf_op jit(solution)/shard_map/ppermute | solution.py:119
  633.9 11.9 %collective-permute-done.43 = bf16[512,768]{1,0:T(8,128)(2,1)S(1)} collective-permute-done((bf16[512,768]{1,0:T(8,128)(2,1)S(1)}, bf16[512,768]{1,0:T(8,128)(2,1)S(1)}, u32[]{:S(2)}, u32[]{:S(2)}) %collective-permute-start.43) | collective-permute-done | bytes 786464 | tf_op jit(solution)/shard_map/ppermute | solution.py:80
  645.8 16.9 %collective-permute-done.46 = bf16[512,768]{1,0:T(8,128)(2,1)S(1)} collective-permute-done((bf16[512,768]{1,0:T(8,128)(2,1)S(1)}, bf16[512,768]{1,0:T(8,128)(2,1)S(1)}, u32[]{:S(2)}, u32[]{:S(2)}) %collective-permute-start.46) | collective-permute-done | bytes 786464 | tf_op jit(solution)/shard_map/ppermute | solution.py:80
  663.1 16.6 %collective-permute-done.47 = bf16[512,768]{1,0:T(8,128)(2,1)S(1)} collective-permute-done((bf16[512,768]{1,0:T(8,128)(2,1)}, bf16[512,768]{1,0:T(8,128)(2,1)S(1)}, u32[]{:S(2)}, u32[]{:S(2)}) %collective-permute-start.47) | collective-permute-done | bytes 786464 | tf_op jit(solution)/shard_map/ppermute | solution.py:80
  679.6 16.6 %collective-permute-done.50 = bf16[512,768]{1,0:T(8,128)(2,1)S(1)} collective-permute-done((bf16[512,768]{1,0:T(8,128)(2,1)S(1)}, bf16[512,768]{1,0:T(8,128)(2,1)S(1)}, u32[]{:S(2)}, u32[]{:S(2)}) %collective-permute-start.50) | collective-permute-done | bytes 786464 | tf_op jit(solution)/shard_map/ppermute | solution.py:80
  722.1 16.5 %collective-permute-done.23 = bf16[128,2048]{1,0:T(8,128)(2,1)S(1)} collective-permute-done((bf16[128,2048]{1,0:T(8,128)(2,1)S(1)}, bf16[128,2048]{1,0:T(8,128)(2,1)S(1)}, u32[]{:S(2)}, u32[]{:S(2)}) %collective-permute-start.23) | collective-permute-done | bytes 524320 | tf_op jit(solution)/shard_map/ppermute | solution.py:80
  761.1 14.4 %collective-permute-done.26 = bf16[128,2048]{1,0:T(8,128)(2,1)S(1)} collective-permute-done((bf16[128,2048]{1,0:T(8,128)(2,1)S(1)}, bf16[128,2048]{1,0:T(8,128)(2,1)S(1)}, u32[]{:S(2)}, u32[]{:S(2)}) %collective-permute-start.26) | collective-permute-done | bytes 524320 | tf_op jit(solution)/shard_map/ppermute | solution.py:80
  795.1 12.1 %shard_map.244 = f32[512,6144]{1,0:T(8,128)} custom-call(bf16[8,512,768]{2,1,0:T(8,128)(2,1)} %bitcast.105), custom_call_target="tpu_custom_call" | custom-call | tf_op jit(solution)/shard_map/pallas_call | solution.py:217
  808.3 11.9 %shard_map.242 = (f32[512,2048]{1,0:T(8,128)}, f32[512,1024]{1,0:T(8,128)}, f32[512,1024]{1,0:T(8,128)}, f32[512,2048]{1,0:T(8,128)}) custom-call(bf16[8,512,768]{2,1,0:T(8,128)(2,1)} %bitcast.104), custom_call_target="tpu_custom_call" | custom-call | tf_op jit(solution)/shard_map/pallas_call | solution.py:217
  820.2 16.4 %shard_map.243 = (f32[512,6144]{1,0:T(8,128)}, f32[512,6144]{1,0:T(8,128)}) custom-call(bf16[8,512,1536]{2,1,0:T(8,128)(2,1)} %bitcast.103), custom_call_target="tpu_custom_call" | custom-call | tf_op jit(solution)/shard_map/pallas_call | solution.py:217
  (345 shorter events, 377.5 us)
Async XLA Ops:
  7.2 64.0 %all-gather.14.cloned.1.call-start = ((), (), s32[]{:S(2)}) async-start(), calls=%async_computation.1 | async-start | bytes 4718592 | tf_op jit(solution)/shard_map/all_gather | solution.py:138
  10.0 114.5 %all-gather.20.cloned.1.call-start = ((), (), s32[]{:S(2)}) async-start(), calls=%async_computation.4 | async-start | bytes 4718592 | tf_op jit(solution)/shard_map/all_gather | solution.py:152
  12.7 45.4 %collective-permute-start.2 = (bf16[528,512]{1,0:T(8,128)(2,1)S(1)}, bf16[528,512]{1,0:T(8,128)(2,1)}, u32[]{:S(2)}, u32[]{:S(2)}) collective-permute-start(bf16[528,512]{1,0:T(8,128)(2,1)S(1)} %pad_maximum_fusion.7.refs_0_), channel_id=1, source_target_pairs={{8,16},{16,8},{9,17},{17,9},{10,18},{18,10},{11,19},{19,11},{12,20... | collective-permute-start | bytes 1622024 | tf_op jit(solution)/shard_map/ppermute | solution.py:105
  87.6 231.0 %all-gather.22.cloned.1.call-start = ((), (), s32[]{:S(2)}) async-start(), calls=%async_computation.5 | async-start | bytes 4718592 | tf_op jit(solution)/shard_map/all_gather | solution.py:152
  136.1 229.6 %all-gather.16.cloned.1.call-start = ((), (), s32[]{:S(2)}) async-start(), calls=%async_computation.2 | async-start | bytes 4718592 | tf_op jit(solution)/shard_map/all_gather | solution.py:138
  140.1 89.0 %collective-permute-start.9 = (bf16[512,1536]{1,0:T(8,128)(2,1)}, bf16[512,1536]{1,0:T(8,128)(2,1)}, u32[]{:S(2)}, u32[]{:S(2)}) collective-permute-start(bf16[512,1536]{1,0:T(8,128)(2,1)} %pad_maximum_fusion.3), channel_id=1, source_target_pairs={{0,16},{8,24},{16,0},{24,8},{1,17},{9,25},{17,1},{25,9},{2,18},{10... | collective-permute-start | bytes 4718600 | tf_op jit(solution)/shard_map/ppermute | solution.py:80
  143.7 102.3 %collective-permute-start.13 = (bf16[512,768]{1,0:T(8,128)(2,1)S(1)}, bf16[512,768]{1,0:T(8,128)(2,1)}, u32[]{:S(2)}, u32[]{:S(2)}) collective-permute-start(bf16[512,768]{1,0:T(8,128)(2,1)S(1)} %constant_dynamic-slice_fusion), channel_id=1, source_target_pairs={{0,16},{8,24},{16,0},{24,8},{1,17},{9,25},{17,1},{25,9},{2,18},{10... | collective-permute-start | bytes 2359304 | tf_op jit(solution)/shard_map/ppermute | solution.py:80
  144.3 108.1 %collective-permute-start.14 = (bf16[512,768]{1,0:T(8,128)(2,1)S(1)}, bf16[512,768]{1,0:T(8,128)(2,1)}, u32[]{:S(2)}, u32[]{:S(2)}) collective-permute-start(bf16[512,768]{1,0:T(8,128)(2,1)S(1)} %constant_dynamic-slice_fusion), channel_id=1, source_target_pairs={{8,16},{16,8},{9,17},{17,9},{10,18},{18,10},{11,19},{19,11},{12,20... | collective-permute-start | bytes 2359304 | tf_op jit(solution)/shard_map/ppermute | solution.py:105
  145.8 170.0 %collective-permute-start.10 = (bf16[512,1536]{1,0:T(8,128)(2,1)}, bf16[512,1536]{1,0:T(8,128)(2,1)}, u32[]{:S(2)}, u32[]{:S(2)}) collective-permute-start(bf16[512,1536]{1,0:T(8,128)(2,1)} %pad_maximum_fusion.3), channel_id=1, source_target_pairs={{8,16},{16,8},{9,17},{17,9},{10,18},{18,10},{11,19},{19,11},{12,20... | collective-permute-start | bytes 4718600 | tf_op jit(solution)/shard_map/ppermute | solution.py:105
  229.1 86.7 %collective-permute-start.11 = (bf16[512,1536]{1,0:T(8,128)(2,1)}, bf16[512,1536]{1,0:T(8,128)(2,1)}, u32[]{:S(2)}, u32[]{:S(2)}) collective-permute-start(bf16[512,1536]{1,0:T(8,128)(2,1)} %collective-permute-done.9), channel_id=1, source_target_pairs={{16,24},{8,0},{17,25},{9,1},{18,26},{10,2},{19,27},{11,3},{20,28},... | collective-permute-start | bytes 4718600 | tf_op jit(solution)/shard_map/ppermute | solution.py:106
  246.0 49.9 %collective-permute-start.15 = (bf16[512,768]{1,0:T(8,128)(2,1)}, bf16[512,768]{1,0:T(8,128)(2,1)}, u32[]{:S(2)}, u32[]{:S(2)}) collective-permute-start(bf16[512,768]{1,0:T(8,128)(2,1)} %collective-permute-done.13), channel_id=1, source_target_pairs={{16,24},{8,0},{17,25},{9,1},{18,26},{10,2},{19,27},{11,3},{20,28},... | collective-permute-start | bytes 2359304 | tf_op jit(solution)/shard_map/ppermute | solution.py:106
  247.5 65.2 %collective-permute-start.12 = (bf16[512,768]{1,0:T(8,128)(2,1)S(1)}, bf16[512,768]{1,0:T(8,128)(2,1)}, u32[]{:S(2)}, u32[]{:S(2)}) collective-permute-start(bf16[512,768]{1,0:T(8,128)(2,1)S(1)} %constant_dynamic-slice_fusion), channel_id=1, source_target_pairs={{0,8},{8,0},{16,24},{24,16},{1,9},{9,1},{17,25},{25,17},{2,10},{10... | collective-permute-start | bytes 2359304 | tf_op jit(solution)/shard_map/ppermute | solution.py:80
  252.4 94.0 %collective-permute-start.8 = (bf16[512,1536]{1,0:T(8,128)(2,1)}, bf16[512,1536]{1,0:T(8,128)(2,1)}, u32[]{:S(2)}, u32[]{:S(2)}) collective-permute-start(bf16[512,1536]{1,0:T(8,128)(2,1)} %pad_maximum_fusion.3), channel_id=1, source_target_pairs={{0,8},{8,0},{16,24},{24,16},{1,9},{9,1},{17,25},{25,17},{2,10},{10... | collective-permute-start | bytes 4718600 | tf_op jit(solution)/shard_map/ppermute | solution.py:80
  377.0 138.1 %all-gather.18.cloned.1.call-start = ((), (), s32[]{:S(2)}) async-start(), calls=%async_computation.3 | async-start | bytes 4718592 | tf_op jit(solution)/shard_map/all_gather | solution.py:138
  453.7 341.4 %all-gather.28.cloned.1.call-start = ((), (), s32[]{:S(2)}) async-start(), calls=%async_computation.8 | async-start | bytes 7077888 | tf_op jit(solution)/shard_map/all_gather | solution.py:214
  513.6 294.7 %all-gather.24.cloned.1.call-start = ((), (), s32[]{:S(2)}) async-start(), calls=%async_computation.6 | async-start | bytes 7077888 | tf_op jit(solution)/shard_map/all_gather | solution.py:214
  591.2 229.0 %all-gather.26.cloned.1.call-start = ((), (), s32[]{:S(2)}) async-start(), calls=%async_computation.7 | async-start | bytes 14155776 | tf_op jit(solution)/shard_map/all_gather | solution.py:214
  596.1 49.7 %collective-permute-start.43 = (bf16[512,768]{1,0:T(8,128)(2,1)S(1)}, bf16[512,768]{1,0:T(8,128)(2,1)S(1)}, u32[]{:S(2)}, u32[]{:S(2)}) collective-permute-start(bf16[512,768]{1,0:T(8,128)(2,1)S(1)} %copy-done.53), channel_id=1, source_target_pairs={{0,8},{8,0},{16,24},{24,16},{1,9},{9,1},{17,25},{25,17},{2,10},{10... | collective-permute-start | bytes 2359304 | tf_op jit(solution)/shard_map/ppermute | solution.py:80
  615.0 47.7 %collective-permute-start.46 = (bf16[512,768]{1,0:T(8,128)(2,1)S(1)}, bf16[512,768]{1,0:T(8,128)(2,1)S(1)}, u32[]{:S(2)}, u32[]{:S(2)}) collective-permute-start(bf16[512,768]{1,0:T(8,128)(2,1)S(1)} %add_convert_fusion.5), channel_id=1, source_target_pairs={{0,16},{8,24},{16,0},{24,8},{1,17},{9,25},{17,1},{25,9},{2,18},{10... | collective-permute-start | bytes 2359304 | tf_op jit(solution)/shard_map/ppermute | solution.py:80
  617.5 45.6 %collective-permute-start.48 = (bf16[512,768]{1,0:T(8,128)(2,1)}, bf16[512,768]{1,0:T(8,128)(2,1)S(1)}, u32[]{:S(2)}, u32[]{:S(2)}) collective-permute-start(bf16[512,768]{1,0:T(8,128)(2,1)} %convolution_convert_fusion.9), channel_id=1, source_target_pairs={{8,16},{16,8},{9,17},{17,9},{10,18},{18,10},{11,19},{19,11},{12,20... | collective-permute-start | bytes 2359304 | tf_op jit(solution)/shard_map/ppermute | solution.py:120
  629.0 50.6 %collective-permute-start.47 = (bf16[512,768]{1,0:T(8,128)(2,1)}, bf16[512,768]{1,0:T(8,128)(2,1)S(1)}, u32[]{:S(2)}, u32[]{:S(2)}) collective-permute-start(bf16[512,768]{1,0:T(8,128)(2,1)} %convolution_convert_fusion.10), channel_id=1, source_target_pairs={{0,8},{8,0},{16,24},{24,16},{1,9},{9,1},{17,25},{25,17},{2,10},{10... | collective-permute-start | bytes 2359304 | tf_op jit(solution)/shard_map/ppermute | solution.py:80
  633.7 62.5 %collective-permute-start.50 = (bf16[512,768]{1,0:T(8,128)(2,1)S(1)}, bf16[512,768]{1,0:T(8,128)(2,1)S(1)}, u32[]{:S(2)}, u32[]{:S(2)}) collective-permute-start(bf16[512,768]{1,0:T(8,128)(2,1)S(1)} %add_convert_fusion.3), channel_id=1, source_target_pairs={{0,16},{8,24},{16,0},{24,8},{1,17},{9,25},{17,1},{25,9},{2,18},{10... | collective-permute-start | bytes 2359304 | tf_op jit(solution)/shard_map/ppermute | solution.py:80
  718.5 42.6 %collective-permute-start.27 = (bf16[128,2048]{1,0:T(8,128)(2,1)S(1)}, bf16[128,2048]{1,0:T(8,128)(2,1)S(1)}, u32[]{:S(2)}, u32[]{:S(2)}) collective-permute-start(bf16[128,2048]{1,0:T(8,128)(2,1)S(1)} %get-tuple-element.79), channel_id=1, source_target_pairs={{0,6},{1,7},{2,4},{3,5},{4,2},{5,3},{6,0},{7,1},{8,14},{9,15},{10,... | collective-permute-start | bytes 1572872 | tf_op jit(solution)/shard_map/ppermute | solution.py:80
  720.9 54.7 %collective-permute-start.26 = (bf16[128,2048]{1,0:T(8,128)(2,1)S(1)}, bf16[128,2048]{1,0:T(8,128)(2,1)S(1)}, u32[]{:S(2)}, u32[]{:S(2)}) collective-permute-start(bf16[128,2048]{1,0:T(8,128)(2,1)S(1)} %get-tuple-element.80), channel_id=1, source_target_pairs={{0,4},{1,5},{2,6},{3,7},{4,0},{5,1},{6,2},{7,3},{8,12},{9,13},{10,... | collective-permute-start | bytes 1572872 | tf_op jit(solution)/shard_map/ppermute | solution.py:80
  (96 other events, 2206.5 us)
Sparse Core Ops, SparseCore 0:
  10.5 39.2 all-gather.13
  87.7 36.6 all-gather.19
  136.2 36.5 all-gather.21
  174.6 36.5 all-gather.15
  453.8 36.2 all-gather.17
  513.8 44.7 all-gather.27
  591.3 45.8 all-gather.23
  698.0 110.0 all-gather.25

commit v3 on v2

--- a/solution.py
+++ b/solution.py
@@ -154,7 +154,7 @@
     order = jnp.arange(plane, dtype=jnp.int32)
     if lines == LINE:
         order = order ^ (lax.axis_index(FSDP) * (plane // lines))
-    tile = 128
+    tile = 256
 
     def from_piece(at):
         return pl.BlockSpec((1, tile, width), lambda row, order: (order[at], row, 0))
@@ -231,6 +231,45 @@
         results.append(jnp.transpose(piece, (1, 0, 2)).reshape(rows, size * width))
         offset = offset + width
     return results
+
+
+def choosing_kernel(spot, mine, other, out):
+    own = pl.program_id(1) % 2 == spot[0] % 2
+
+    @pl.when(own)
+    def _():
+        out[...] = mine[0].astype(out.dtype)
+
+    @pl.when(jnp.logical_not(own))
+    def _():
+        out[...] = other[0].astype(out.dtype)
+
+
+def spread_direct(reduced):
+    size = lax.axis_size(SP)
+    rows, width = reduced.shape
+    if size != PLANE:
+        return spread(reduced, [width])[0]
+    found = [reduced]
+    for turn in (1, 2, 3):
+        found.append(flip_permute(reduced, SP, 2 * turn))
+    mine = jnp.stack(found)
+    other = flip_permute(mine, SP, 1)
+    spot = lax.axis_index(SP).astype(jnp.int32)[None]
+    tile = 256
+    piece = pl.BlockSpec(
+        (1, tile, width), lambda row, at, spot: ((at // 2) ^ (spot[0] // 2), row, 0)
+    )
+    return pl.pallas_call(
+        choosing_kernel,
+        out_shape=jax.ShapeDtypeStruct((rows, size * width), single_precision),
+        grid_spec=pltpu.PrefetchScalarGridSpec(
+            num_scalar_prefetch=1,
+            grid=(rows // tile, size),
+            in_specs=[piece, piece],
+            out_specs=pl.BlockSpec((tile, width), lambda row, at, spot: (row, at)),
+        ),
+    )(spot, mine, other)
 
 
 def projecting_kernel(heads, count, x, gain, query_gain, key_gain, cosine, sine, *refs):
@@ -593,7 +632,7 @@
     ).astype(reduced_precision)
     up_grads = (hidden_grad * silu_val).astype(reduced_precision)
     both_grads = jnp.concatenate([gate_grad, up_grads], axis=1)
-    out_pieces, _ = tie(jnp.concatenate(line_order(out_blocks), axis=0), second_norm)
+    out_pieces, _ = tie(jnp.concatenate(line_order(out_blocks), axis=0), both_grads)
     out_rows = lax.all_to_all(
         out_pieces.reshape(plane, query_width, model_cols),
         SP,
@@ -601,8 +640,8 @@
         concat_axis=0,
         tiled=True,
     )
-    both_grads, out_rows = tie(both_grads, out_rows)
     norm_two_part = contract_last(both_grads, gate_up).astype(reduced_precision)
+    norm_two_part, out_rows = tie(norm_two_part, out_rows)
     norm_two_grad = plane_reduce(norm_two_part.reshape(plane, token_rows, model_width))
     gate_parts = row_parts(second_norm, both_grads[:, :ff_cols])
     up_parts = row_parts(second_norm, both_grads[:, ff_cols:])
@@ -616,8 +655,7 @@
     )
     half = middle_grad.astype(reduced_precision)
     half_all = plane_rows(half)
-    late_hidden, _ = tie(hidden, half)
-    block_part = contract_last(late_hidden, down_cols).astype(reduced_precision)
+    block_part = contract_last(hidden, down_cols).astype(reduced_precision)
     block_out = line_columns(
         (
             middle_own + plane_reduce(block_part.reshape(plane, token_rows, model_width))
@@ -710,7 +748,8 @@
     grad_postnorm = small[row_block : 2 * row_block]
     grad_querynorm = small[2 * row_block : 2 * row_block + HEAD_DIMENSION]
     grad_keynorm = small[2 * row_block + HEAD_DIMENSION :]
-    grad_down, grad_gate = spread(jnp.concatenate([down_sum, gate_sum], axis=1), [ff_cols, ff_cols])
+    grad_down = spread_direct(down_sum)
+    grad_gate = spread_direct(gate_sum)
     (grad_up,) = spread(up_sum, [ff_cols])
     grad_query, grad_key, grad_value, grad_output = spread(
         jnp.concatenate([qkv_sum, out_sum], axis=1), [query_width, owned, owned, model_cols]

time: 855 us -> 872 us (1.020)
  starting transfers between devices: 95.2 us -> 109 us
  Pallas kernels: 85.3 us -> 94.4 us
    pallas_call x0 -> x2, Pallas kernels: none -> 29.3 us  [spread_direct(): pl.pallas_call(choosing_kernel, out_shape=jax.ShapeDtypeStruct((rows, siz...]
    ppermute x35 -> x43, starting transfers between devices: 62.3 us -> 78.7 us  [flip_permute(): return lax.ppermute(piece, axis, [(i, i ^ flip) for i in range(size)])]
    pallas_call x3 -> x2, Pallas kernels: 40.4 us -> 24.1 us  [spread(): pl.pallas_call(functools.partial(widening_kernel, widths), grid=(rows //...]
    ppermute x4, waiting for transfers between devices: 49.3 us -> 62.8 us  [line_gather(): outer = lax.ppermute(second, FSDP, [(2, 3), (1, 0)])]
    ppermute x35 -> x43, waiting for transfers between devices: 366 us -> 357 us  [flip_permute(): return lax.ppermute(piece, axis, [(i, i ^ flip) for i in range(size)])]
  transfers between devices with their start and end apart: 64 -> 71, of which waited for: 34 -> 37; matrix products, arithmetic and copies ran while one was open for 15% -> 17% of each run, Pallas kernels for 5% -> 7%
where the time goes in v3:
time: 872 us; the launch traced here: 861 us
  waiting for transfers between devices  480 us (55%)
  starting transfers between devices  109 us (12%)
  matrix products  94.7 us (11%)
  Pallas kernels  94.4 us (11%)
  other arithmetic  42.5 us (5%)
  local copies, waits for them, and re-layouts  24.7 us (3%)
  between operations  15.9 us (2%)
    ppermute x43, waiting for transfers between devices, flip_permute(): return lax.ppermute(piece, axis, [(i, i ^ flip) for i in range(size)])  357 us
    ppermute x43, starting transfers between devices, flip_permute(): return lax.ppermute(piece, axis, [(i, i ^ flip) for i in range(size)])  78.7 us
    ppermute x4, waiting for transfers between devices, line_gather(): outer = lax.ppermute(second, FSDP, [(2, 3), (1, 0)])  62.8 us
    ppermute x6, waiting for transfers between devices, line_reduce(): outer = lax.ppermute(parts[3], FSDP, [(3, 2), (0, 1)])  48.4 us
    dot_general x20, matrix products, contract_first(): lax.dot_general(left_side, right_side, (((0,), (0,)), ((), ())), preferre...  39.7 us
    dot_general x4, matrix products, contract_last(): lax.dot_general(left_side, right_side, (((1,), (1,)), ((), ())), preferre...  31.8 us
    pallas_call x2, Pallas kernels, spread_direct(): pl.pallas_call(choosing_kernel, out_shape=jax.ShapeDtypeStruct((rows, siz...  29.3 us
    pallas_call x2, Pallas kernels, spread(): pl.pallas_call(functools.partial(widening_kernel, widths), grid=(rows //...  24.1 us
  transfers between devices with their start and end apart: 71, of which 37 were waited for; matrix products, arithmetic and copies ran while one was open for 17% of the time, Pallas kernels for 7%

profile of v3, /device:TPU:0, one launch (start us, length us, event | category | flops | bytes accessed | tf_op | source)
XLA Modules:
  0.0 860.8 jit_solution(10777016917938745205)
XLA Ops:
  23.6 30.7 %collective-permute-done.1.refs_2_ = bf16[528,512]{1,0:T(8,128)(2,1)S(1)} collective-permute-done((bf16[528,512]{1,0:T(8,128)(2,1)S(1)}, bf16[528,512]{1,0:T(8,128)(2,1)S(1)}, u32[]{:S(2)}, u32[]{:S(2)}) %collective-permute-start.1) | collective-permute-done | bytes 540704 | tf_op jit(solution)/shard_map/ppermute | solution.py:80
  58.1 11.2 %collective-permute-done.3 = bf16[528,512]{1,0:T(8,128)(2,1)S(1)} collective-permute-done((bf16[528,512]{1,0:T(8,128)(2,1)S(1)}, bf16[528,512]{1,0:T(8,128)(2,1)S(1)}, u32[]{:S(2)}, u32[]{:S(2)}) %collective-permute-start.3) | collective-permute-done | bytes 540704 | tf_op jit(solution)/shard_map/ppermute | solution.py:106
  112.1 11.8 %all-gather.18.cloned.1.call-done = bf16[8192,256]{1,0:T(8,128)(2,1)} async-done(((bf16[1024,256]{1,0:T(8,128)(2,1)}), bf16[8192,256]{1,0:T(8,128)(2,1)}) %all-gather.18.cloned.1.call-update) | async-done | bytes 4194320 | tf_op jit(solution)/shard_map/all_gather | solution.py:152
  145.2 81.5 %collective-permute-done.9 = bf16[512,1536]{1,0:T(8,128)(2,1)} collective-permute-done((bf16[512,1536]{1,0:T(8,128)(2,1)}, bf16[512,1536]{1,0:T(8,128)(2,1)}, u32[]{:S(2)}, u32[]{:S(2)}) %collective-permute-start.9) | collective-permute-done | bytes 1572896 | tf_op jit(solution)/shard_map/ppermute | solution.py:80
  231.8 11.8 %collective-permute-done.13 = bf16[512,768]{1,0:T(8,128)(2,1)} collective-permute-done((bf16[512,768]{1,0:T(8,128)(2,1)S(1)}, bf16[512,768]{1,0:T(8,128)(2,1)}, u32[]{:S(2)}, u32[]{:S(2)}) %collective-permute-start.13) | collective-permute-done | bytes 786464 | tf_op jit(solution)/shard_map/ppermute | solution.py:80
  246.1 14.9 %collective-permute-start.8 = (bf16[512,1536]{1,0:T(8,128)(2,1)}, bf16[512,1536]{1,0:T(8,128)(2,1)}, u32[]{:S(2)}, u32[]{:S(2)}) collective-permute-start(bf16[512,1536]{1,0:T(8,128)(2,1)} %pad_maximum_fusion.5), channel_id=1, source_target_pairs={{0,8},{8,0},{16,24},{24,16},{1,9},{9,1},{17,25},{25,17},{2,10},{10... | collective-permute-start | bytes 4718600 | tf_op jit(solution)/shard_map/ppermute | solution.py:80
  266.6 43.7 %collective-permute-done.15 = bf16[512,768]{1,0:T(8,128)(2,1)} collective-permute-done((bf16[512,768]{1,0:T(8,128)(2,1)}, bf16[512,768]{1,0:T(8,128)(2,1)}, u32[]{:S(2)}, u32[]{:S(2)}) %collective-permute-start.15) | collective-permute-done | bytes 786464 | tf_op jit(solution)/shard_map/ppermute | solution.py:106
  324.4 19.6 %collective-permute-done.8 = bf16[512,1536]{1,0:T(8,128)(2,1)} collective-permute-done((bf16[512,1536]{1,0:T(8,128)(2,1)}, bf16[512,1536]{1,0:T(8,128)(2,1)}, u32[]{:S(2)}, u32[]{:S(2)}) %collective-permute-start.8) | collective-permute-done | bytes 1572896 | tf_op jit(solution)/shard_map/ppermute | solution.py:80
  344.0 14.5 %fusion.111 = f32[1024,1536]{1,0:T(8,128)S(1)} fusion(bf16[1024,2048]{1,0:T(8,128)(2,1)} %get-tuple-element.37, bf16[512,1536]{1,0:T(8,128)(2,1)} %broadcast_select_fusion, bf16[512,1536]{1,0:T(8,128)(2,1)} %collective-permute-done.9, bf16[512,1536]{1,0:T(8,128)(2,1)} %collective-permute-done.8, bf16[512,768]{1,0:T(8,128)(2,1)S(1)} %get-tuple-element.128, ...), kind=kOutput, calls=%fused_computation.272 | convolution fusion | flops 6473908224 | bytes 16777216 | tf_op jit(solution)/shard_map/dot_general | solution.py:39
  376.3 16.0 %convolution_convert_fusion = bf16[1024,2048]{1,0:T(8,128)(2,1)} fusion(bf16[512,1536]{1,0:T(8,128)(2,1)S(1)} %copy-done.20, bf16[512,1536]{1,0:T(8,128)(2,1)} %collective-permute-done.9, bf16[512,1536]{1,0:T(8,128)(2,1)} %collective-permute-done.8, bf16[512,768]{1,0:T(8,128)(2,1)S(1)} %get-tuple-element.128, bf16[512,768]{1,0:T(8,128)(2,1)S(1)} %copy-done.11, ...), kind=kOutput, calls=%fused_computation.8 | convolution fusion | flops 6482296832 | bytes 13631488 | tf_op jit(solution)/shard_map/dot_general | solution.py:27
  453.1 11.3 %collective-permute-done.19 = bf16[128,2048]{1,0:T(8,128)(2,1)S(1)} collective-permute-done((bf16[128,2048]{1,0:T(8,128)(2,1)S(1)}, bf16[128,2048]{1,0:T(8,128)(2,1)S(1)}, u32[]{:S(2)}, u32[]{:S(2)}) %collective-permute-start.19) | collective-permute-done | bytes 524320 | tf_op jit(solution)/shard_map/ppermute | solution.py:80
  470.8 17.4 %collective-permute-done.53 = bf16[512,768]{1,0:T(8,128)(2,1)S(1)} collective-permute-done((bf16[512,768]{1,0:T(8,128)(2,1)}, bf16[512,768]{1,0:T(8,128)(2,1)S(1)}, u32[]{:S(2)}, u32[]{:S(2)}) %collective-permute-start.53) | collective-permute-done | bytes 786464 | tf_op jit(solution)/shard_map/ppermute | solution.py:119
  505.1 19.9 %collective-permute-done.54 = bf16[512,768]{1,0:T(8,128)(2,1)S(1)} collective-permute-done((bf16[512,768]{1,0:T(8,128)(2,1)S(1)}, bf16[512,768]{1,0:T(8,128)(2,1)S(1)}, u32[]{:S(2)}, u32[]{:S(2)}) %collective-permute-start.54) | collective-permute-done | bytes 786464 | tf_op jit(solution)/shard_map/ppermute | solution.py:80
  537.6 12.1 %shard_map.241 = (bf16[1024,256]{1,0:T(8,128)(2,1)}, bf16[1024,128]{1,0:T(8,128)(2,1)}, bf16[1024,128]{1,0:T(8,128)(2,1)}, f32[1,128]{1,0:T(1,128)}, f32[1,128]{1,0:T(1,128)}) custom-call(bf16[1024,512]{1,0:T(8,128)(2,1)} %get-tuple-element.34.query.key.value, bf16[1024,512]{1,0:T(8,128)(2,1)} %get-tuple-element.34.query.key.value, ...), custom_call_target="tpu_custom_call" | custom-call | tf_op jit(solution)/shard_map/pallas_call | solution.py:475
  592.5 11.9 %collective-permute-done.38 = bf16[512,512]{1,0:T(8,128)(2,1)S(1)} collective-permute-done((bf16[512,512]{1,0:T(8,128)(2,1)S(1)}, bf16[512,512]{1,0:T(8,128)(2,1)S(1)}, u32[]{:S(2)}, u32[]{:S(2)}) %collective-permute-start.38) | collective-permute-done | bytes 524320 | tf_op jit(solution)/shard_map/ppermute | solution.py:80
  613.8 12.1 %collective-permute-done.45 = bf16[512,768]{1,0:T(8,128)(2,1)S(1)} collective-permute-done((bf16[512,768]{1,0:T(8,128)(2,1)}, bf16[512,768]{1,0:T(8,128)(2,1)S(1)}, u32[]{:S(2)}, u32[]{:S(2)}) %collective-permute-start.45) | collective-permute-done | bytes 786464 | tf_op jit(solution)/shard_map/ppermute | solution.py:119
  629.6 13.1 %collective-permute-done.57 = bf16[512,768]{1,0:T(8,128)(2,1)S(1)} collective-permute-done((bf16[512,768]{1,0:T(8,128)(2,1)}, bf16[512,768]{1,0:T(8,128)(2,1)S(1)}, u32[]{:S(2)}, u32[]{:S(2)}) %collective-permute-start.57) | collective-permute-done | bytes 786464 | tf_op jit(solution)/shard_map/ppermute | solution.py:119
  647.5 12.0 %collective-permute-done.43 = bf16[512,768]{1,0:T(8,128)(2,1)S(1)} collective-permute-done((bf16[512,768]{1,0:T(8,128)(2,1)}, bf16[512,768]{1,0:T(8,128)(2,1)S(1)}, u32[]{:S(2)}, u32[]{:S(2)}) %collective-permute-start.43) | collective-permute-done | bytes 786464 | tf_op jit(solution)/shard_map/ppermute | solution.py:80
  662.2 31.0 %collective-permute-done.46 = bf16[512,768]{1,0:T(8,128)(2,1)S(1)} collective-permute-done((bf16[512,768]{1,0:T(8,128)(2,1)S(1)}, bf16[512,768]{1,0:T(8,128)(2,1)S(1)}, u32[]{:S(2)}, u32[]{:S(2)}) %collective-permute-start.46) | collective-permute-done | bytes 786464 | tf_op jit(solution)/shard_map/ppermute | solution.py:80
  718.5 12.4 %collective-permute-done.48 = bf16[512,768]{1,0:T(8,128)(2,1)S(1)} collective-permute-done((bf16[512,768]{1,0:T(8,128)(2,1)S(1)}, bf16[512,768]{1,0:T(8,128)(2,1)S(1)}, u32[]{:S(2)}, u32[]{:S(2)}) %collective-permute-start.48) | collective-permute-done | bytes 786464 | tf_op jit(solution)/shard_map/ppermute | solution.py:80
  781.2 14.6 %shard_map.243 = f32[512,6144]{1,0:T(8,128)} custom-call(s32[1]{0:T(128)} %bitcast.35.spot, bf16[4,512,768]{2,1,0:T(8,128)(2,1)} %copy-done.2, bf16[4,512,768]{2,1,0:T(8,128)(2,1)} %copy-done.12), custom_call_target="tpu_custom_call" | custom-call | tf_op jit(solution)/shard_map/pallas_call | solution.py:263
  795.9 14.7 %shard_map.245 = f32[512,6144]{1,0:T(8,128)} custom-call(s32[1]{0:T(128)} %bitcast.35.spot, bf16[4,512,768]{2,1,0:T(8,128)(2,1)} %pad_maximum_fusion.4.mine, bf16[4,512,768]{2,1,0:T(8,128)(2,1)} %collective-permute-done.62.other), custom_call_target="tpu_custom_call" | custom-call | tf_op jit(solution)/shard_map/pallas_call | solution.py:263
  828.2 12.1 %shard_map.244 = f32[512,6144]{1,0:T(8,128)} custom-call(bf16[8,512,768]{2,1,0:T(8,128)(2,1)} %bitcast.119), custom_call_target="tpu_custom_call" | custom-call | tf_op jit(solution)/shard_map/pallas_call | solution.py:217
  841.4 12.1 %shard_map.242 = (f32[512,2048]{1,0:T(8,128)}, f32[512,1024]{1,0:T(8,128)}, f32[512,1024]{1,0:T(8,128)}, f32[512,2048]{1,0:T(8,128)}) custom-call(bf16[8,512,768]{2,1,0:T(8,128)(2,1)} %bitcast.118), custom_call_target="tpu_custom_call" | custom-call | tf_op jit(solution)/shard_map/pallas_call | solution.py:217
  (379 shorter events, 382.5 us)
Async XLA Ops:
  7.2 63.5 %all-gather.12.cloned.1.call-start = ((), (), s32[]{:S(2)}) async-start(), calls=%async_computation.1 | async-start | bytes 4718592 | tf_op jit(solution)/shard_map/all_gather | solution.py:138
  10.0 113.9 %all-gather.18.cloned.1.call-start = ((), (), s32[]{:S(2)}) async-start(), calls=%async_computation.4 | async-start | bytes 4718592 | tf_op jit(solution)/shard_map/all_gather | solution.py:152
  87.0 230.3 %all-gather.20.cloned.1.call-start = ((), (), s32[]{:S(2)}) async-start(), calls=%async_computation.5 | async-start | bytes 4718592 | tf_op jit(solution)/shard_map/all_gather | solution.py:152
  133.8 229.5 %all-gather.14.cloned.1.call-start = ((), (), s32[]{:S(2)}) async-start(), calls=%async_computation.2 | async-start | bytes 4718592 | tf_op jit(solution)/shard_map/all_gather | solution.py:138
  137.7 89.0 %collective-permute-start.9 = (bf16[512,1536]{1,0:T(8,128)(2,1)}, bf16[512,1536]{1,0:T(8,128)(2,1)}, u32[]{:S(2)}, u32[]{:S(2)}) collective-permute-start(bf16[512,1536]{1,0:T(8,128)(2,1)} %pad_maximum_fusion.5), channel_id=1, source_target_pairs={{0,16},{8,24},{16,0},{24,8},{1,17},{9,25},{17,1},{25,9},{2,18},{10... | collective-permute-start | bytes 4718600 | tf_op jit(solution)/shard_map/ppermute | solution.py:80
  141.3 102.3 %collective-permute-start.13 = (bf16[512,768]{1,0:T(8,128)(2,1)S(1)}, bf16[512,768]{1,0:T(8,128)(2,1)}, u32[]{:S(2)}, u32[]{:S(2)}) collective-permute-start(bf16[512,768]{1,0:T(8,128)(2,1)S(1)} %constant_dynamic-slice_fusion), channel_id=1, source_target_pairs={{0,16},{8,24},{16,0},{24,8},{1,17},{9,25},{17,1},{25,9},{2,18},{10... | collective-permute-start | bytes 2359304 | tf_op jit(solution)/shard_map/ppermute | solution.py:80
  141.9 104.2 %collective-permute-start.14 = (bf16[512,768]{1,0:T(8,128)(2,1)S(1)}, bf16[512,768]{1,0:T(8,128)(2,1)}, u32[]{:S(2)}, u32[]{:S(2)}) collective-permute-start(bf16[512,768]{1,0:T(8,128)(2,1)S(1)} %constant_dynamic-slice_fusion), channel_id=1, source_target_pairs={{8,16},{16,8},{9,17},{17,9},{10,18},{18,10},{11,19},{19,11},{12,20... | collective-permute-start | bytes 2359304 | tf_op jit(solution)/shard_map/ppermute | solution.py:105
  143.4 171.2 %collective-permute-start.10 = (bf16[512,1536]{1,0:T(8,128)(2,1)}, bf16[512,1536]{1,0:T(8,128)(2,1)}, u32[]{:S(2)}, u32[]{:S(2)}) collective-permute-start(bf16[512,1536]{1,0:T(8,128)(2,1)} %pad_maximum_fusion.5), channel_id=1, source_target_pairs={{8,16},{16,8},{9,17},{17,9},{10,18},{18,10},{11,19},{19,11},{12,20... | collective-permute-start | bytes 4718600 | tf_op jit(solution)/shard_map/ppermute | solution.py:105
  226.7 87.9 %collective-permute-start.11 = (bf16[512,1536]{1,0:T(8,128)(2,1)}, bf16[512,1536]{1,0:T(8,128)(2,1)}, u32[]{:S(2)}, u32[]{:S(2)}) collective-permute-start(bf16[512,1536]{1,0:T(8,128)(2,1)} %collective-permute-done.9), channel_id=1, source_target_pairs={{16,24},{8,0},{17,25},{9,1},{18,26},{10,2},{19,27},{11,3},{20,28},... | collective-permute-start | bytes 4718600 | tf_op jit(solution)/shard_map/ppermute | solution.py:106
  228.0 83.6 %collective-permute-start.12 = (bf16[512,768]{1,0:T(8,128)(2,1)S(1)}, bf16[512,768]{1,0:T(8,128)(2,1)}, u32[]{:S(2)}, u32[]{:S(2)}) collective-permute-start(bf16[512,768]{1,0:T(8,128)(2,1)S(1)} %constant_dynamic-slice_fusion), channel_id=1, source_target_pairs={{0,8},{8,0},{16,24},{24,16},{1,9},{9,1},{17,25},{25,17},{2,10},{10... | collective-permute-start | bytes 2359304 | tf_op jit(solution)/shard_map/ppermute | solution.py:80
  243.6 66.7 %collective-permute-start.15 = (bf16[512,768]{1,0:T(8,128)(2,1)}, bf16[512,768]{1,0:T(8,128)(2,1)}, u32[]{:S(2)}, u32[]{:S(2)}) collective-permute-start(bf16[512,768]{1,0:T(8,128)(2,1)} %collective-permute-done.13), channel_id=1, source_target_pairs={{16,24},{8,0},{17,25},{9,1},{18,26},{10,2},{19,27},{11,3},{20,28},... | collective-permute-start | bytes 2359304 | tf_op jit(solution)/shard_map/ppermute | solution.py:106
  246.1 97.9 %collective-permute-start.8 = (bf16[512,1536]{1,0:T(8,128)(2,1)}, bf16[512,1536]{1,0:T(8,128)(2,1)}, u32[]{:S(2)}, u32[]{:S(2)}) collective-permute-start(bf16[512,1536]{1,0:T(8,128)(2,1)} %pad_maximum_fusion.5), channel_id=1, source_target_pairs={{0,8},{8,0},{16,24},{24,16},{1,9},{9,1},{17,25},{25,17},{2,10},{10... | collective-permute-start | bytes 4718600 | tf_op jit(solution)/shard_map/ppermute | solution.py:80
  262.2 135.4 %all-to-all-start = ((bf16[8,256,256]{2,1,0:T(8,128)(2,1)}), bf16[8,256,256]{2,1,0:T(8,128)(2,1)S(1)}, u32[]{:S(2)}, u32[]{:S(2)}) async-start(bf16[8,256,256]{2,1,0:T(8,128)(2,1)} %bitcast.13), calls=%async_computation | async-start | bytes 2097152 | tf_op jit(solution)/shard_map/all_to_all | solution.py:636
  265.7 261.6 %all-gather.16.cloned.1.call-start = ((), (), s32[]{:S(2)}) async-start(), calls=%async_computation.3 | async-start | bytes 4718592 | tf_op jit(solution)/shard_map/all_gather | solution.py:138
  468.5 359.7 %all-gather.24.cloned.1.call-start = ((), (), s32[]{:S(2)}) async-start(), calls=%async_computation.7 | async-start | bytes 7077888 | tf_op jit(solution)/shard_map/all_gather | solution.py:214
  526.4 315.0 %all-gather.22.cloned.1.call-start = ((), (), s32[]{:S(2)}) async-start(), calls=%async_computation.6 | async-start | bytes 7077888 | tf_op jit(solution)/shard_map/all_gather | solution.py:214
  532.3 49.9 %collective-permute-start.40 = (bf16[512,256]{1,0:T(8,128)(2,1)}, bf16[512,256]{1,0:T(8,128)(2,1)S(1)}, u32[]{:S(2)}, u32[]{:S(2)}) collective-permute-start(bf16[512,256]{1,0:T(8,128)(2,1)} %convolution_convert_fusion.21), channel_id=1, source_target_pairs={{8,16},{16,8},{9,17},{17,9},{10,18},{18,10},{11,19},{19,11},{12,20... | collective-permute-start | bytes 786440 | tf_op jit(solution)/shard_map/ppermute | solution.py:120
  609.1 50.5 %collective-permute-start.43 = (bf16[512,768]{1,0:T(8,128)(2,1)}, bf16[512,768]{1,0:T(8,128)(2,1)S(1)}, u32[]{:S(2)}, u32[]{:S(2)}) collective-permute-start(bf16[512,768]{1,0:T(8,128)(2,1)} %convolution_convert_fusion.10), channel_id=1, source_target_pairs={{0,8},{8,0},{16,24},{24,16},{1,9},{9,1},{17,25},{25,17},{2,10},{10... | collective-permute-start | bytes 2359304 | tf_op jit(solution)/shard_map/ppermute | solution.py:80
  609.1 53.1 %collective-permute-start.44 = (bf16[512,768]{1,0:T(8,128)(2,1)}, bf16[512,768]{1,0:T(8,128)(2,1)S(1)}, u32[]{:S(2)}, u32[]{:S(2)}) collective-permute-start(bf16[512,768]{1,0:T(8,128)(2,1)} %convolution_convert_fusion.9), channel_id=1, source_target_pairs={{8,16},{16,8},{9,17},{17,9},{10,18},{18,10},{11,19},{19,11},{12,20... | collective-permute-start | bytes 2359304 | tf_op jit(solution)/shard_map/ppermute | solution.py:120
  609.8 85.7 %collective-permute-start.55 = (bf16[512,768]{1,0:T(8,128)(2,1)}, bf16[512,768]{1,0:T(8,128)(2,1)S(1)}, u32[]{:S(2)}, u32[]{:S(2)}) collective-permute-start(bf16[512,768]{1,0:T(8,128)(2,1)} %convolution_convert_fusion.13), channel_id=1, source_target_pairs={{0,8},{8,0},{16,24},{24,16},{1,9},{9,1},{17,25},{25,17},{2,10},{10... | collective-permute-start | bytes 2359304 | tf_op jit(solution)/shard_map/ppermute | solution.py:80
  625.9 71.3 %collective-permute-start.56 = (bf16[512,768]{1,0:T(8,128)(2,1)}, bf16[512,768]{1,0:T(8,128)(2,1)S(1)}, u32[]{:S(2)}, u32[]{:S(2)}) collective-permute-start(bf16[512,768]{1,0:T(8,128)(2,1)} %convolution_convert_fusion.12), channel_id=1, source_target_pairs={{8,16},{16,8},{9,17},{17,9},{10,18},{18,10},{11,19},{19,11},{12,20... | collective-permute-start | bytes 2359304 | tf_op jit(solution)/shard_map/ppermute | solution.py:120
  642.7 50.5 %collective-permute-start.46 = (bf16[512,768]{1,0:T(8,128)(2,1)S(1)}, bf16[512,768]{1,0:T(8,128)(2,1)S(1)}, u32[]{:S(2)}, u32[]{:S(2)}) collective-permute-start(bf16[512,768]{1,0:T(8,128)(2,1)S(1)} %add_convert_fusion.5), channel_id=1, source_target_pairs={{0,16},{8,24},{16,0},{24,8},{1,17},{9,25},{17,1},{25,9},{2,18},{10... | collective-permute-start | bytes 2359304 | tf_op jit(solution)/shard_map/ppermute | solution.py:80
  659.6 48.7 %collective-permute-start.58 = (bf16[512,768]{1,0:T(8,128)(2,1)S(1)}, bf16[512,768]{1,0:T(8,128)(2,1)S(1)}, u32[]{:S(2)}, u32[]{:S(2)}) collective-permute-start(bf16[512,768]{1,0:T(8,128)(2,1)S(1)} %add_convert_fusion.1), channel_id=1, source_target_pairs={{0,16},{8,24},{16,0},{24,8},{1,17},{9,25},{17,1},{25,9},{2,18},{10... | collective-permute-start | bytes 2359304 | tf_op jit(solution)/shard_map/ppermute | solution.py:80
  731.4 48.1 %collective-permute-start.50 = (bf16[4,512,768]{2,1,0:T(8,128)(2,1)S(1)}, bf16[4,512,768]{2,1,0:T(8,128)(2,1)S(1)}, u32[]{:S(2)}, u32[]{:S(2)}) collective-permute-start(bf16[4,512,768]{2,1,0:T(8,128)(2,1)S(1)} %pad_maximum_fusion.3.mine), channel_id=1, source_target_pairs={{0,1},{1,0},{2,3},{3,2},{4,5},{5,4},{6,7},{7,6},{8,9},{9,8},{10,11... | collective-permute-start | bytes 9437192 | tf_op jit(solution)/shard_map/ppermute | solution.py:80
  (113 other events, 2886.8 us)
Sparse Core Ops, SparseCore 0:
  10.5 39.2 all-gather.11
  87.2 36.6 all-gather.17
  133.9 36.5 all-gather.19
  172.3 36.5 all-gather.13
  468.6 36.7 all-gather.15
  526.5 44.8 all-gather.23
  606.3 43.2 all-gather.21
